TPU v7x, 32 devices: a whole 2x2x4 slice. The times are simulated.
32 devices in a mesh: batch: 4 (over y, core), seq: 8 (over z, x).
Axes of the slice: x: 2, y: 2, z: 4, core: 2. Of those that a mesh axis runs over, the one named last changes fastest.
Arguments:
- tokens: bfloat16 [4, 1024, 2048], P('batch', 'seq'), may hold values from -6 to 6
- lengths: int32 [4], P('batch'), may hold values from 256 to 1024, as said below
- norm_gain: bfloat16 [2048], P(('batch', 'seq')), may hold values from 0.5 to 1.5
- in_proj: bfloat16 [2048, 8192], P(('batch', 'seq')), may hold values from -0.125 to 0.125
- conv_weight: bfloat16 [4, 4096], P(None, ('batch', 'seq')), may hold values from -3 to 3
- conv_bias: bfloat16 [4096], P(('batch', 'seq')), may hold values from -3 to 3
- x_proj: bfloat16 [4096, 160], P(('batch', 'seq')), may hold values from -0.09375 to 0.09375
- dt_proj: bfloat16 [128, 4096], P(None, ('batch', 'seq')), may hold values from -0.25 to 0.25
- dt_bias: bfloat16 [4096], P(('batch', 'seq')), may hold values from -12 to 0
- a_log: bfloat16 [4096, 16], P(('batch', 'seq')), may hold values from 0 to 2.6875
- skip: bfloat16 [4096], P(('batch', 'seq')), may hold values from 0.5 to 1.5
- out_proj: bfloat16 [4096, 2048], P(('batch', 'seq')), may hold values from -0.375 to 0.375
- cotangent: bfloat16 [4, 1024, 2048], P('batch', 'seq'), may hold values from -6 to 6
Outputs:
- block_out: float32 [4, 1024, 2048], P('batch', 'seq')
- grad_tokens: float32 [4, 1024, 2048], P('batch', 'seq')
- grad_norm_gain: float32 [2048], P(('batch', 'seq'))
- grad_in_proj: float32 [2048, 8192], P(('batch', 'seq'))
- grad_conv_weight: float32 [4, 4096], P(None, ('batch', 'seq'))
- grad_conv_bias: float32 [4096], P(('batch', 'seq'))
- grad_x_proj: float32 [4096, 160], P(('batch', 'seq'))
- grad_dt_proj: float32 [128, 4096], P(None, ('batch', 'seq'))
- grad_dt_bias: float32 [4096], P(('batch', 'seq'))
- grad_a_log: float32 [4096, 16], P(('batch', 'seq'))
- grad_skip: float32 [4096], P(('batch', 'seq'))
- grad_out_proj: float32 [4096, 2048], P(('batch', 'seq'))
Inputs may be any that keep to these rules, and one draw needn't show every extreme that they name: Slots below lengths[i] of sequence i hold tokens, the rest are padding; in every draw one sequence has exactly 1024 slots and one exactly a quarter of 1024.
All inputs are finite; a program needn't handle non-finite values.
Results may differ from a plain program's by a relative error of at most 0.012.
Values may be sent and summed in bfloat16 or wider, within the bound.
No kernel may reach another device: no remote copies, remote signals or barrier semaphores. Data moves between devices by JAX's collectives and lax.ppermute only.
A program may use at most 448 MiB of HBM per device.

v0:
```python
import functools

import jax
import jax.numpy as jnp
from jax import lax
from jax.experimental import pallas as pl
from jax.experimental.pallas import tpu as pltpu
from jax.sharding import PartitionSpec as P

bf16, f32 = jnp.bfloat16, jnp.float32
NT = (((1,), (1,)), ((), ()))
LANES = 128
GROUP = 32
BLOCK = 128
epsilon = 1e-05
LOG2E = 1.4426950408889634


def spread(tile, row, lanes, states):
    return jnp.broadcast_to(tile[row : row + 1, lanes], (states, LANES))


def selectors(select, states):
    low = select.shape[1] - 4 * states
    middle = low + 2 * states
    block = select[:, low:middle].astype(f32) + select[:, middle:].astype(f32)
    return jnp.transpose(block), block[:, :states], block[:, states:]


def block_diagonal(values, step):
    rows, states = values.shape
    wide = step * states
    spread_out = (
        lax.broadcasted_iota(jnp.int32, (states, wide), 1) % states
        == lax.broadcasted_iota(jnp.int32, (states, wide), 0)
    ).astype(bf16)
    value = jnp.dot(values.astype(bf16), spread_out, preferred_element_type=f32)
    place = lax.broadcasted_iota(jnp.int32, (rows, wide), 0) % step
    owner = lax.broadcasted_iota(jnp.int32, (rows, wide), 1) // states
    return jnp.where(place == owner, value, 0.0).astype(bf16)


def forward_body(tiles, step, delta, active, select, rate, mixed, kept, state, drive, columns):
    rows, states = delta.shape[0], rate.shape[0]
    wide = step * states

    @pl.when(pl.program_id(0) == 0)
    def _():
        state[...] = jnp.zeros_like(state)

    turned, _, c_block = selectors(select[...], states)
    columns[...] = turned[:states]
    drive[...] = delta[...] * active[...].astype(f32)
    rates = [rate[:, k * LANES : (k + 1) * LANES] for k in range(tiles)]

    def group(number, held):
        held = list(held)
        base = pl.multiple_of(number * GROUP, GROUP)
        delta_now, drive_now = delta.at[pl.ds(base, GROUP), :], drive.at[pl.ds(base, GROUP), :]
        b_now = pltpu.roll(columns[...], rows - base, 1)
        for j in range(GROUP):
            b_wide = jnp.broadcast_to(b_now[:, j : j + 1], (states, LANES))
            for k in range(tiles):
                lanes = slice(k * LANES, (k + 1) * LANES)
                decay = jnp.exp2(spread(delta_now, j, lanes, states) * rates[k])
                held[k] = decay * held[k] + spread(drive_now, j, lanes, states) * b_wide
                at = pl.ds(pl.multiple_of((base + j) * states, states), states)
                kept[at, lanes] = held[k].astype(bf16)
        return tuple(held)

    held = lax.fori_loop(
        0,
        rows // GROUP,
        group,
        tuple(state[:, k * LANES : (k + 1) * LANES] for k in range(tiles)),
    )
    for k in range(tiles):
        state[:, k * LANES : (k + 1) * LANES] = held[k]
    c_diag = block_diagonal(c_block, step)
    for q in range(rows // step):
        part = kept[q * wide : (q + 1) * wide, :]
        spot = slice(q * step, (q + 1) * step)
        mixed[spot, :] = jnp.dot(c_diag[spot, :], part, preferred_element_type=f32)


def scan_forward(delta, active, select, rate, block, step):
    length, width = delta.shape
    states = rate.shape[0]
    tiles = width // LANES
    return pl.pallas_call(
        functools.partial(forward_body, tiles, step),
        grid=(length // block,),
        in_specs=[
            pl.BlockSpec((block, width), lambda i: (i, 0)),
            pl.BlockSpec((block, width), lambda i: (i, 0)),
            pl.BlockSpec((block, select.shape[1]), lambda i: (i, 0)),
            pl.BlockSpec((states, width), lambda i: (0, 0)),
        ],
        out_specs=[
            pl.BlockSpec((block, width), lambda i: (i, 0)),
            pl.BlockSpec((block * states, width), lambda i: (i, 0)),
        ],
        out_shape=[
            jax.ShapeDtypeStruct((length, width), f32),
            jax.ShapeDtypeStruct((length * states, width), bf16),
        ],
        scratch_shapes=[
            pltpu.VMEM((states, width), f32),
            pltpu.VMEM((block, width), f32),
            pltpu.VMEM((states, block), f32),
        ],
        compiler_params=pltpu.CompilerParams(vmem_limit_bytes=48 << 20),
        cost_estimate=pl.CostEstimate(
            flops=8 * length * width * states,
            transcendentals=length * width * states,
            bytes_accessed=length * width * (2 * states + 10),
        ),
        name="scan_forward",
    )(delta, active, select, rate)


FEW = 4


def backward_body(
    tiles, step, delta, active, d_mixed, select, rate, decay_rate, kept, kept_before,
    d_delta, d_active, d_bc, d_log, push, drive, columns, diagonals, folding, timed, *pairs,
):
    grads, rated = pairs[:2], pairs[2:]
    rows, states = delta.shape[0], rate.shape[0]
    blocks = pl.num_programs(0)
    first = pl.program_id(0) == blocks - 1
    wide = step * states

    @pl.when(pl.program_id(0) == 0)
    def _():
        push[...] = jnp.zeros_like(push)
        d_log[...] = jnp.zeros_like(d_log)

    turned, b_block, _ = selectors(select[...], states)
    columns[...] = turned[states:]
    drive[...] = delta[...] * active[...].astype(f32)
    rates = [rate[:, k * LANES : (k + 1) * LANES] for k in range(tiles)]
    own_rates = [decay_rate[:, k * LANES : (k + 1) * LANES].astype(bf16) for k in range(tiles)]

    place = lax.broadcasted_iota(jnp.int32, (step, wide), 0)
    owner = lax.broadcasted_iota(jnp.int32, (step, wide), 1) // states
    ones_diag = (place == owner).astype(bf16)
    diag = (place == owner).astype(f32)
    diagonals[...] = block_diagonal(b_block, step)

    def sums_of(number):
        held, through_of = number % 2, {}

        def spots(q):
            at = number * GROUP + q * step
            tall = slice(q * wide, (q + 1) * wide)
            return slice(at, at + step), tall

        def through(q):
            spot, tall = spots(q)
            value = jnp.dot(diagonals[spot, :], grads[held][tall, :], preferred_element_type=f32)
            d_active[spot, :] = delta[spot, :] * value
            through_of[q] = active[spot, :].astype(f32) * value

        def summed(q):
            spot, tall = spots(q)
            value = jnp.dot(ones_diag, rated[held][tall, :], preferred_element_type=f32)
            d_delta[spot, :] = value + through_of[q]

        def d_b(q):
            spot, tall = spots(q)
            folding[spot, :wide] = diag * lax.dot_general(
                drive[spot, :].astype(bf16), grads[held][tall, :], NT, preferred_element_type=f32
            )

        def d_c(q):
            spot, _ = spots(q)
            own = slice(spot.start * states, spot.stop * states)
            folding[spot, wide:] = diag * lax.dot_general(
                d_mixed[spot, :].astype(bf16), kept[own, :], NT, preferred_element_type=f32
            )

        return [
            functools.partial(part, q)
            for q in range(GROUP // step)
            for part in (through, summed, d_b, d_c)
        ]

    carry = [push[:, k * LANES : (k + 1) * LANES] for k in range(tiles)]
    waiting = []
    for number in reversed(range(rows // GROUP)):
        pace = GROUP // max(len(waiting), 1)
        sums = [None] * tiles
        held = number % 2
        for j in reversed(range(GROUP)):
            row = number * GROUP + j
            c_wide = jnp.broadcast_to(columns[:, row : row + 1], (states, LANES))
            at = slice(j * states, (j + 1) * states)
            for k in range(tiles):
                lanes = slice(k * LANES, (k + 1) * LANES)
                if row:
                    before = kept[(row - 1) * states : row * states, lanes]
                else:
                    before = jnp.where(first, jnp.zeros((), bf16), kept_before[:, lanes])
                step_size = spread(delta, row, lanes, states)
                grad = spread(d_mixed, row, lanes, states) * c_wide + carry[k]
                carry[k] = jnp.exp2(step_size * rates[k]) * grad
                grads[held][at, lanes] = grad.astype(bf16)
                rated_now = carry[k].astype(bf16) * before * own_rates[k]
                rated[held][at, lanes] = rated_now
                timed_now = rated_now * step_size.astype(bf16)
                sums[k] = timed_now if sums[k] is None else sums[k] + timed_now
                if j % FEW == 0:
                    spot = row // FEW * states
                    timed[spot : spot + states, lanes] = sums[k]
                    sums[k] = None
            if waiting and j % pace == 0:
                waiting.pop(0)()
        while waiting:
            waiting.pop(0)()
        waiting = sums_of(number)
    while waiting:
        waiting.pop(0)()
    for k in range(tiles):
        push[:, k * LANES : (k + 1) * LANES] = carry[k]
    fold = (
        lax.broadcasted_iota(jnp.int32, (wide, states), 0) % states
        == lax.broadcasted_iota(jnp.int32, (wide, states), 1)
    ).astype(bf16)
    for number in range(2):
        value = folding[:, number * wide : (number + 1) * wide]
        high = value.astype(bf16)
        d_bc[:, number * states : (number + 1) * states] = jnp.dot(
            high, fold, preferred_element_type=f32
        )
    span = rows // FEW * states
    pick = (
        lax.broadcasted_iota(jnp.int32, (states, span), 1) % states
        == lax.broadcasted_iota(jnp.int32, (states, span), 0)
    ).astype(bf16)
    d_log[...] += jnp.dot(pick, timed[...], preferred_element_type=f32)


def scan_backward(delta, active, d_mixed, select, rate, decay_rate, kept, block, step):
    length, width = delta.shape
    states = rate.shape[0]
    tiles = width // LANES
    blocks = length // block
    back = lambda i: (blocks - 1 - i, 0)
    return pl.pallas_call(
        functools.partial(backward_body, tiles, step),
        grid=(blocks,),
        in_specs=[
            pl.BlockSpec((block, width), back),
            pl.BlockSpec((block, width), back),
            pl.BlockSpec((block, width), back),
            pl.BlockSpec((block, select.shape[1]), back),
            pl.BlockSpec((states, width), lambda i: (0, 0)),
            pl.BlockSpec((states, width), lambda i: (0, 0)),
            pl.BlockSpec((block * states, width), back),
            pl.BlockSpec(
                (states, width), lambda i: (jnp.maximum((blocks - 1 - i) * block - 1, 0), 0)
            ),
        ],
        out_specs=[
            pl.BlockSpec((block, width), back),
            pl.BlockSpec((block, width), back),
            pl.BlockSpec((block, 2 * states), back),
            pl.BlockSpec((states, width), lambda i: (0, 0)),
        ],
        out_shape=[
            jax.ShapeDtypeStruct((length, width), f32),
            jax.ShapeDtypeStruct((length, width), f32),
            jax.ShapeDtypeStruct((length, 2 * states), f32),
            jax.ShapeDtypeStruct((states, width), f32),
        ],
        scratch_shapes=[
            pltpu.VMEM((states, width), f32),
            pltpu.VMEM((block, width), f32),
            pltpu.VMEM((states, block), f32),
            pltpu.VMEM((block, step * states), bf16),
            pltpu.VMEM((block, 2 * step * states), f32),
            pltpu.VMEM((block // FEW * states, width), bf16),
        ]
        + [pltpu.VMEM((GROUP * states, width), bf16)] * 4,
        compiler_params=pltpu.CompilerParams(vmem_limit_bytes=48 << 20),
        cost_estimate=pl.CostEstimate(
            flops=20 * length * width * states,
            transcendentals=length * width * states,
            bytes_accessed=length * width * (2 * states + 20),
        ),
        name="scan_backward",
    )(delta, active, d_mixed, select, rate, decay_rate, kept, kept)


together = lax.optimization_barrier


def inner_swap(value, axis):
    count = lax.axis_size(axis)
    return lax.ppermute(value, axis, [(i, i ^ 1) for i in range(count)])


def outer_shift(value, axis, steps):
    count = lax.axis_size(axis)
    half = count // 2
    pairs = [(i, (i // 2 + steps) % half * 2 + i % 2) for i in range(count)]
    return lax.ppermute(value, axis, pairs)


def shift_order(half):
    return sorted(range(1, half), key=lambda k: (-min(k, half - k), k))


def pieces_of_all(own, axis):
    count = lax.axis_size(axis)
    place = lax.axis_index(axis)
    half = count // 2
    outer, inner = place // 2, place % 2
    yield place, own
    arrived = {k: outer_shift(own, axis, k) for k in shift_order(half)}
    yield outer * 2 + 1 - inner, inner_swap(own, axis)
    for k, piece in arrived.items():
        origin = (outer - k + half) % half
        yield origin * 2 + inner, piece
    for k, piece in arrived.items():
        origin = (outer - k + half) % half
        yield origin * 2 + 1 - inner, inner_swap(piece, axis)


def gathered(own, axis, dim=0):
    count, size = lax.axis_size(axis), own.shape[dim]
    whole = jnp.zeros(own.shape[:dim] + (count * size,) + own.shape[dim + 1 :], own.dtype)
    for place, piece in pieces_of_all(own, axis):
        whole = lax.dynamic_update_slice_in_dim(whole, piece, place * size, dim)
    return whole


def hop(value, axis, moves):
    pairs = [(a * 2 + i, b * 2 + i) for a, b in moves for i in (0, 1)]
    return lax.ppermute(value, axis, pairs)


def swap_at(value, axis, spots):
    pairs = [(a * 2 + i, a * 2 + 1 - i) for a in spots for i in (0, 1)]
    return lax.ppermute(value, axis, pairs)


UP, DOWN = [(0, 1), (1, 2), (2, 3)], [(1, 0), (2, 1), (3, 2)]


def line_gathered(own, axis):
    if lax.axis_size(axis) != 8:
        return lax.all_gather(own, axis, axis=0, tiled=True)
    place = lax.axis_index(axis)
    z, x = place // 2, place % 2
    rows = own.shape[0]
    upper, edge = z >= 2, (z == 0) | (z == 3)
    across = jnp.where(upper, z - 2, z + 2)
    far = jnp.where(z == 3, 0, 3)

    def put(whole, piece, spot, side):
        return lax.dynamic_update_slice_in_dim(whole, piece, (spot * 2 + side) * rows, 0)

    def put_far(whole, piece, side):
        held = lax.dynamic_slice_in_dim(whole, (far * 2 + side) * rows, rows, 0)
        return put(whole, jnp.where(edge, piece, held), far, side)

    whole = jnp.zeros((8 * rows,) + own.shape[1:], own.dtype)
    up, down, other = hop(own, axis, UP), hop(own, axis, DOWN), swap_at(own, axis, range(4))
    up_two, down_two = hop(up, axis, UP[1:]), hop(down, axis, DOWN[:2])
    other_up, other_down = swap_at(up, axis, (1, 2, 3)), swap_at(down, axis, (0, 1, 2))
    whole = put(put(whole, own, z, x), other, z, 1 - x)
    whole = put(put(whole, up, (z + 3) % 4, x), down, (z + 1) % 4, x)
    two = jnp.where(upper, up_two, down_two)
    three = hop(two, axis, [(2, 3), (1, 0)])
    other_two = swap_at(two, axis, range(4))
    whole = put(put(whole, other_up, (z + 3) % 4, 1 - x), other_down, (z + 1) % 4, 1 - x)
    whole = put(whole, two, across, x)
    other_three = swap_at(three, axis, (0, 3))
    whole = put(whole, other_two, across, 1 - x)
    return put_far(put_far(whole, three, x), other_three, 1 - x)


def line_summed(part_of, axis):
    if lax.axis_size(axis) != 8:
        return (scattered_sum(part_of, axis),)
    place = lax.axis_index(axis)
    z, x = place // 2, place % 2
    upper, edge = z >= 2, (z == 0) | (z == 3)
    across = jnp.where(upper, z - 2, z + 2)
    far = jnp.where(z == 0, 3, 0)
    above, below = jnp.minimum(z + 1, 3), jnp.maximum(z - 1, 0)

    def swapped(spot, spots):
        return swap_at(part_of(spot * 2 + 1 - x), axis, spots)

    def added(spot, given):
        return part_of(spot * 2 + x).astype(f32) + given.astype(f32)

    given_far = swapped(far, (0, 3))
    given_across = swapped(across, range(4))
    given_above, given_below = swapped(above, (0, 1, 2)), swapped(below, (1, 2, 3))
    given_own = swapped(z, range(4))
    three = hop(added(far, given_far).astype(bf16), axis, [(0, 1), (3, 2)])
    three, given_across, given_above, given_below = together(
        (three, given_across, given_above, given_below)
    )
    two = added(across, given_across) + jnp.where(edge, 0.0, three.astype(f32))
    two = two.astype(bf16)
    two_up, two_down, given_own = together(
        (hop(two, axis, UP[:2]), hop(two, axis, DOWN[1:]), given_own)
    )
    one_up = (added(above, given_above) + two_up.astype(f32)).astype(bf16)
    one_down = (added(below, given_below) + two_down.astype(f32)).astype(bf16)
    return added(z, given_own), hop(one_up, axis, UP), hop(one_down, axis, DOWN)


def scattered_sum(part_of, axis):
    count = lax.axis_size(axis)
    place = lax.axis_index(axis)
    half = count // 2
    outer, inner = place // 2, place % 2
    total = None
    for k in shift_order(half) + [0]:
        target = (outer + k) % half
        given = inner_swap(part_of(target * 2 + 1 - inner), axis)
        piece = part_of(target * 2 + inner).astype(f32) + given.astype(f32)
        if k:
            piece = outer_shift(piece.astype(bf16), axis, k).astype(f32)
        total = piece if total is None else total + piece
    return total


def rows_of(value, rows):
    return lambda place: lax.dynamic_slice_in_dim(value, place * rows, rows, 0)


def summed_over_seq(part, change):
    count = lax.axis_size("seq")
    length, columns = part.shape
    part = part.astype(bf16).reshape(count, length // count, columns)
    own = change(jnp.sum(lax.all_to_all(part, "seq", 0, 0).astype(f32), axis=0))
    return shared(own, "seq").reshape(length, own.shape[1])


def two_terms(value):
    high = value.astype(bf16)
    return [high, (value - high.astype(f32)).astype(bf16)]


def shared(own, axis):
    wide = jnp.broadcast_to(own[None], (lax.axis_size(axis),) + own.shape)
    return lax.all_to_all(wide, axis, 0, 0)


def matmul(a, b, dims=(((1,), (0,)), ((), ()))):
    return lax.dot_general(a, b, dims, preferred_element_type=f32)


TN = (((0,), (0,)), ((), ()))


def on_device(
    tokens,
    lengths,
    norm_gain,
    in_proj,
    conv_weight,
    conv_bias,
    x_proj,
    dt_proj,
    dt_bias,
    a_log,
    skip,
    out_proj,
    cotangent,
):
    batch, seq = lax.axis_size("batch"), lax.axis_size("seq")
    place = lax.axis_index("seq")
    span, model = tokens.shape[1:]
    length = span * seq
    in_rows = in_proj.shape[0]
    own = skip.shape[0]
    taps = conv_weight.shape[0]
    rank = dt_proj.shape[0]
    states = a_log.shape[1]
    width = own * batch

    halves = in_proj.reshape(in_rows, 2, batch, seq, own).transpose(1, 3, 0, 2, 4)
    halves = halves.reshape(2, seq, in_rows, width)
    columns = lax.all_to_all(halves[0], "seq", 0, 0)
    small = jnp.concatenate(
        [
            dt_proj,
            x_proj.T,
            a_log.T,
            conv_weight,
            conv_bias[None],
            dt_bias[None],
            skip[None],
            jnp.pad(norm_gain, (0, own - in_rows))[None],
        ],
        axis=0,
    )
    small = gathered(small, "batch", 1)
    cuts = [rank, 2 * rank + 2 * states, 2 * rank + 3 * states]
    cuts = cuts + [cuts[2] + taps + i for i in range(4)]
    delta_weight, select_weight, decay_logs, conv_taps, conv_shift, delta_shift, skip_gain, gain = (
        jnp.split(small, cuts, axis=0)
    )
    conv_taps, conv_shift = conv_taps.astype(f32), conv_shift.astype(f32)
    delta_shift, skip_gain = delta_shift.astype(f32), skip_gain.astype(f32)
    decay = -jnp.exp(decay_logs.astype(f32))
    gain = gain.reshape(batch, own)[:, :in_rows]
    columns, gain = together((columns, gain))
    gain = shared(gain, "seq")
    gate_columns, gain = together((halves[1], gain))
    gate_columns = lax.all_to_all(gate_columns, "seq", 0, 0)
    gain = gain.transpose(1, 0, 2).reshape(model).astype(f32)

    input_weight = gathered(columns.reshape(seq * in_rows, width), "batch")
    output_weight = gathered(out_proj, "batch")

    def normed(rows):
        rows = rows.astype(f32)
        scale = lax.rsqrt(jnp.mean(rows * rows, axis=-1, keepdims=True) + epsilon)
        return (rows * scale * gain).astype(bf16)

    stream = lax.all_gather(tokens[0], "seq", axis=0, tiled=True)
    gate_weight = gathered(gate_columns.reshape(seq * in_rows, width), "batch")
    normalized = normed(stream)
    upstream = line_gathered(cotangent[0], "seq")

    valid = (jnp.arange(length, dtype=jnp.int32) < lengths[0])[:, None]
    inner = matmul(normalized, input_weight).astype(bf16)
    padded = jnp.pad(inner, ((taps - 1, 0), (0, 0)))
    conv_out = conv_shift + jnp.zeros((length, width), f32)
    for tap in range(taps):
        conv_out = conv_out + conv_taps[tap] * padded[tap : tap + length].astype(f32)
    active = jax.nn.silu(conv_out).astype(bf16)
    active_f = active.astype(f32)

    partial, upstream = together((matmul(active, select_weight, NT), upstream))
    select = summed_over_seq(
        partial,
        lambda s: jnp.concatenate([s[:, :rank].astype(bf16)] + two_terms(s[:, rank:]), axis=1),
    )
    upstream = jnp.where(valid, upstream, 0).astype(bf16)
    gate_low = matmul(normalized, gate_weight).astype(bf16)
    d_gated = matmul(upstream, output_weight, NT)
    select, gate_low, d_gated = together((select, gate_low, d_gated))
    gate = gate_low.astype(f32)
    gate_sig = jax.nn.sigmoid(gate)
    delta_low = select[:, :rank]
    delta_raw = matmul(delta_low, delta_weight) + delta_shift
    delta = jax.nn.softplus(delta_raw)

    block = min(BLOCK, length)
    step = 256 // states
    rate = decay * LOG2E
    mixed, kept = scan_forward(delta, active, select, rate, block, step)
    mixed = mixed + skip_gain * active_f
    gated = (mixed * gate * gate_sig).astype(bf16)
    branch = matmul(gated, output_weight).astype(bf16)
    d_gated, branch = together((d_gated, branch))
    branch = lax.psum_scatter(branch, "seq", scatter_dimension=0, tiled=True)
    own_valid = lax.dynamic_slice_in_dim(valid, place * span, span, 0)
    own_stream = tokens[0].astype(f32)
    block_out = jnp.where(own_valid, own_stream + branch.astype(f32), 0.0)

    d_mixed = d_gated * gate * gate_sig
    d_gate = d_gated * mixed * gate_sig * (1.0 + gate * (1.0 - gate_sig))
    grad_skip = jnp.sum(d_mixed * active_f, axis=0, keepdims=True)
    d_gate_low = d_gate.astype(bf16)

    d_delta, d_active, d_bc, grad_log = scan_backward(
        delta, active, d_mixed, select, rate, decay, kept, block, step
    )
    d_raw = d_delta * jax.nn.sigmoid(delta_raw)
    grad_dt_bias = jnp.sum(d_raw, axis=0, keepdims=True)
    d_raw_low = d_raw.astype(bf16)
    grad_dt_proj = matmul(delta_low, d_raw_low, TN)
    partial = jnp.concatenate([matmul(d_raw_low, delta_weight, NT), d_bc], axis=1)
    d_select = summed_over_seq(partial, lambda s: s.astype(bf16))
    grad_gate = scattered_sum(
        rows_of(matmul(normalized, d_gate_low, TN).astype(bf16), model // batch), "batch"
    )
    d_select, branch, grad_gate = together((d_select, branch, grad_gate))
    grad_x_proj = matmul(d_select, active, TN)
    d_active = d_active + d_mixed * skip_gain + matmul(d_select, select_weight)
    conv_sig = jax.nn.sigmoid(conv_out)
    d_conv = (d_active * conv_sig * (1.0 + conv_out * (1.0 - conv_sig))).astype(bf16)
    d_conv_f = d_conv.astype(f32)
    grad_conv_bias = jnp.sum(d_conv_f, axis=0, keepdims=True)
    grad_conv = jnp.stack(
        [
            jnp.sum(d_conv_f * padded[tap : tap + length].astype(f32), axis=0)
            for tap in range(taps)
        ]
    )
    extended = jnp.pad(d_conv, ((0, taps - 1), (0, 0)))
    d_inner = jnp.zeros((length, width), f32)
    for tap in range(taps):
        offset = taps - 1 - tap
        d_inner = d_inner + conv_taps[tap] * extended[offset : offset + length].astype(f32)
    d_inner = d_inner.astype(bf16)
    grad_inner = matmul(normalized, d_inner, TN).astype(bf16)
    d_inner, grad_inner = together((d_inner, grad_inner))
    d_normalized = matmul(
        jnp.concatenate([d_inner, d_gate_low], axis=1),
        jnp.concatenate([input_weight, gate_weight], axis=1),
        NT,
    ).astype(bf16)
    grad_inner = scattered_sum(rows_of(grad_inner, model // batch), "batch")
    d_normalized, gated = together((d_normalized, gated))
    grad_output = lax.psum_scatter(
        matmul(gated, upstream, TN).astype(bf16), "batch", scatter_dimension=0, tiled=True
    ).astype(f32)
    d_normalized, *last_terms = line_summed(rows_of(d_normalized, span), "seq")

    both = jnp.concatenate([grad_inner, grad_gate], axis=1).astype(bf16)
    both = lax.all_to_all(both.reshape(seq, in_rows, 2 * width), "seq", 0, 0)
    both = both.reshape(seq, in_rows, 2, batch, own).transpose(1, 2, 3, 0, 4)
    grad_input = both.reshape(in_rows, 2 * batch * seq * own).astype(f32)

    small_grads = jnp.concatenate(
        [grad_dt_proj, grad_x_proj, grad_log, grad_conv, grad_conv_bias, grad_dt_bias, grad_skip],
        axis=0,
    )
    small_grads = lax.psum_scatter(small_grads, "batch", scatter_dimension=1, tiled=True)
    g_dt_proj, g_x_proj, g_log, g_conv, g_conv_bias, g_dt_bias, g_skip = jnp.split(
        small_grads, cuts[:-1], axis=0
    )

    own_upstream = jnp.where(own_valid, cotangent[0].astype(f32), 0.0)
    own_scale = lax.rsqrt(jnp.mean(own_stream * own_stream, axis=-1, keepdims=True) + epsilon)
    grad_gain = jnp.sum(grad_input * in_proj.astype(f32), axis=1) / norm_gain.astype(f32)
    (
        d_normalized, g_dt_proj, g_x_proj, g_log, g_conv, g_conv_bias, g_dt_bias, g_skip,
        grad_input, grad_gain,
    ) = together(
        (
            d_normalized, g_dt_proj, g_x_proj, g_log, g_conv, g_conv_bias, g_dt_bias, g_skip,
            grad_input, grad_gain,
        )
    )
    for term in last_terms:
        d_normalized = d_normalized + term.astype(f32)
    d_hat = d_normalized * gain
    grad_tokens = (
        own_scale * d_hat
        - own_stream
        * own_scale
        * own_scale
        * own_scale
        * jnp.mean(d_hat * own_stream, axis=-1, keepdims=True)
        + own_upstream
    )
    return (
        block_out[None],
        grad_tokens[None],
        grad_gain,
        grad_input,
        g_conv,
        g_conv_bias[0],
        g_x_proj.T,
        g_dt_proj,
        g_dt_bias[0],
        g_log.T,
        g_skip[0],
        grad_output,
    )


def solution(mesh):
    placed = (
        P("batch", "seq", None),
        P("batch"),
        P(("batch", "seq")),
        P(("batch", "seq"), None),
        P(None, ("batch", "seq")),
        P(("batch", "seq")),
        P(("batch", "seq"), None),
        P(None, ("batch", "seq")),
        P(("batch", "seq")),
        P(("batch", "seq"), None),
        P(("batch", "seq")),
        P(("batch", "seq"), None),
        P("batch", "seq", None),
    )
    return jax.shard_map(
        on_device,
        mesh=mesh,
        in_specs=placed,
        out_specs=(
            P("batch", "seq", None),
            P("batch", "seq", None),
            P(("batch", "seq")),
            P(("batch", "seq"), None),
            P(None, ("batch", "seq")),
            P(("batch", "seq")),
            P(("batch", "seq"), None),
            P(None, ("batch", "seq")),
            P(("batch", "seq")),
            P(("batch", "seq"), None),
            P(("batch", "seq")),
            P(("batch", "seq"), None),
        ),
        check_vma=False,
    )
```

profile of v0, /device:TPU:0, one launch (start us, length us, event | category | flops | bytes accessed | tf_op | source)
XLA Modules:
  0.0 470.7 jit_solution(16998610982287072482)
XLA Ops:
  8.6 5.3 %concatenate.33 = bf16[312,128]{1,0:T(8,128)(2,1)} concatenate(bf16[128,128]{1,0:T(8,128)(2,1)} %param.20, bf16[160,128]{1,0:T(8,128)(2,1)} %bitcast.141, bf16[16,128]{1,0:T(8,128)(2,1)} %bitcast.159, bf16[4,128]{1,0:T(4,128)(2,1)} %param.17, bf16[1,128]{1,0:T(2,128)(2,1)} %bitcast.161, bf16[1,128]{1,0:T(2,128)(2,1)} %bitcast.162, bf16[1,128]{1,0:T(2,128)(2,1)} %bitcast.163, ...), dimensions={0} | concatenate | bytes 159744 | tf_op jit(solution)/shard_map/concatenate | solution.py:494
  17.4 4.5 collective-permute-start.7
  47.3 13.9 %collective-permute-done.8 = bf16[128,2048]{1,0:T(8,128)(2,1)} collective-permute-done((bf16[128,2048]{1,0:T(8,128)(2,1)S(1)}, bf16[128,2048]{1,0:T(8,128)(2,1)}, u32[]{:S(2)}, u32[]{:S(2)}) %collective-permute-start.8) | collective-permute-done | bytes 524320 | tf_op jit(solution)/shard_map/ppermute | solution.py:342
  74.1 7.9 %all-to-all-start.1 = ((bf16[8,2,128]{2,1,0:T(2,128)(2,1)}), bf16[8,2,128]{2,1,0:T(2,128)(2,1)}, u32[]{:S(2)}, u32[]{:S(2)}) async-start(bf16[8,2,128]{2,1,0:T(2,128)(2,1)} %reshape.120), calls=%async_computation.1 | async-start | bytes 8192 | tf_op jit(solution)/shard_map/all_to_all | solution.py:455
  85.5 7.0 %collective-permute-done.10 = bf16[128,2048]{1,0:T(8,128)(2,1)} collective-permute-done((bf16[128,2048]{1,0:T(8,128)(2,1)}, bf16[128,2048]{1,0:T(8,128)(2,1)}, u32[]{:S(2)}, u32[]{:S(2)}) %collective-permute-start.10) | collective-permute-done | bytes 524320 | tf_op jit(solution)/shard_map/ppermute | solution.py:347
  104.1 18.1 %all-to-all-start.4 = ((bf16[8,64,512]{2,1,0:T(8,128)(2,1)}), bf16[8,64,512]{2,1,0:T(8,128)(2,1)}, u32[]{:S(2)}, u32[]{:S(2)}) async-start(bf16[8,64,512]{2,1,0:T(8,128)(2,1)} %squeeze.28), calls=%async_computation.4 | async-start | bytes 1048576 | tf_op jit(solution)/shard_map/all_to_all | solution.py:520
  125.1 12.4 %collective-permute-done.14 = bf16[128,2048]{1,0:T(8,128)(2,1)} collective-permute-done((bf16[128,2048]{1,0:T(8,128)(2,1)}, bf16[128,2048]{1,0:T(8,128)(2,1)}, u32[]{:S(2)}, u32[]{:S(2)}) %collective-permute-start.14) | collective-permute-done | bytes 524320 | tf_op jit(solution)/shard_map/ppermute | solution.py:342
  148.4 4.8 %collective-permute-done.15 = bf16[128,2048]{1,0:T(8,128)(2,1)S(1)} collective-permute-done((bf16[128,2048]{1,0:T(8,128)(2,1)}, bf16[128,2048]{1,0:T(8,128)(2,1)S(1)}, u32[]{:S(2)}, u32[]{:S(2)}) %collective-permute-start.15) | collective-permute-done | bytes 524320 | tf_op jit(solution)/shard_map/ppermute | solution.py:347
  185.6 15.6 %all-to-all-start.3 = ((bf16[8,128,192]{1,2,0:T(8,128)(2,1)}), bf16[8,128,192]{1,2,0:T(8,128)(2,1)}, u32[]{:S(2)}, u32[]{:S(2)}) async-start(bf16[8,128,192]{1,2,0:T(8,128)(2,1)} %broadcast_in_dim.96), calls=%async_computation.3 | async-start | bytes 786432 | tf_op jit(solution)/shard_map/all_to_all | solution.py:455
  201.3 6.0 %fusion.34 = f32[1024,512]{1,0:T(8,128)} fusion(bf16[512,2048]{1,0:T(8,128)(2,1)S(1)} %constant_dynamic-update-slice_fusion, bf16[1024,2048]{1,0:T(8,128)(2,1)} %select_dynamic-update-slice_fusion, pred[1024]{0:T(1024)(128)(4,1)} %iota_compare_fusion), kind=kOutput, calls=%fused_computation.66 | convolution fusion | flops 2149580800 | bytes 8389632 | tf_op jit(solution)/shard_map/dot_general | solution.py:459
  207.3 4.9 %convolution_convert_fusion.4 = bf16[1024,512]{1,0:T(8,128)(2,1)} fusion(bf16[2048,512]{1,0:T(8,128)(2,1)} %constant_dynamic-update-slice_fusion.4, bf16[1,1024,2048]{2,1,0:T(8,128)(2,1)S(1)} %copy-done.10, f32[2048]{0:T(1024)S(1)} %reshape.111, f32[1024]{0:T(1024)S(1)} %copy-done.41), kind=kOutput, calls=%fused_computation.67 | convolution fusion | flops 2156396544 | bytes 7352320 | tf_op jit(solution)/shard_map/dot_general | solution.py:459
  219.0 16.4 %scan_forward.1 = (f32[1024,512]{1,0:T(8,128)S(1)}, bf16[16384,512]{1,0:T(8,128)(2,1)}) custom-call(f32[1024,512]{1,0:T(8,128)S(1)} %get-tuple-element.138.delta, bf16[1024,512]{1,0:T(8,128)(2,1)S(1)} %multiply_convert_fusion.1.active, bf16[1024,192]{1,0:T(8,128)(2,1)S(1)} %bitcast.101, f32[16,512]{1,0:T(8,128)S(1)} %get-tuple-element.126.rate), custom_call_target="tpu_custom_call" | custom-call | flops 67108864 | bytes 22020096 | tf_op jit(solution)/shard_map/scan_forward/pallas_call | solution.py:90
  243.1 6.7 %fusion.15 = (f32[512]{0:T(512)}, f32[1024,512]{1,0:T(8,128)}, bf16[1024,512]{1,0:T(8,128)(2,1)S(1)}) fusion(f32[1024,512]{1,0:T(8,128)} %fusion.34, bf16[1024,512]{1,0:T(8,128)(2,1)} %convolution_convert_fusion.4, f32[1024,512]{1,0:T(8,128)S(1)} %get-tuple-element.60, f32[512]{0:T(512)S(1)} %bitcast.147, bf16[1024,512]{1,0:T(8,128)(2,1)} %copy-done.4, ...), kind=kLoop, calls=%fused_computation.37 | loop fusion | flops 18349568 | bytes 9451520 | tf_op jit(solution)/shard_map/reduce_sum | solution.py:575
  254.2 31.0 %scan_backward.1 = (f32[1024,512]{1,0:T(8,128)S(1)}, f32[1024,512]{1,0:T(8,128)}, f32[1024,32]{1,0:T(8,128)S(1)}, f32[16,512]{1,0:T(8,128)S(1)}) custom-call(f32[1024,512]{1,0:T(8,128)} %copy-done.3, bf16[1024,512]{1,0:T(8,128)(2,1)S(1)} %multiply_convert_fusion.1.active, f32[1024,512]{1,0:T(8,128)} %get-tuple-element.100.d_mixed, ...), custom_call_target="tpu_custom_call" | custom-call | flops 167772160 | bytes 27262976 | tf_op jit(solution)/shard_map/scan_backward/pallas_call | solution.py:251
  289.9 5.4 %all-to-all-start.5 = ((bf16[8,128,160]{1,2,0:T(8,128)(2,1)}), bf16[8,128,160]{1,2,0:T(8,128)(2,1)S(1)}, u32[]{:S(2)}, u32[]{:S(2)}) async-start(bf16[8,128,160]{1,2,0:T(8,128)(2,1)} %pad_maximum_fusion.1), calls=%async_computation.6 | async-start | bytes 655360 | tf_op jit(solution)/shard_map/all_to_all | solution.py:444
  298.9 6.7 %all-to-all-done.5 = bf16[8,128,160]{1,2,0:T(8,128)(2,1)S(1)} async-done(((bf16[8,128,160]{1,2,0:T(8,128)(2,1)}), bf16[8,128,160]{1,2,0:T(8,128)(2,1)S(1)}, u32[]{:S(2)}, u32[]{:S(2)}) %all-to-all-start.5) | async-done | bytes 327712 | tf_op jit(solution)/shard_map/all_to_all | solution.py:444
  314.4 9.9 %all-to-all-done.6 = bf16[8,128,160]{1,2,0:T(8,128)(2,1)S(1)} async-done(((bf16[8,128,160]{1,2,0:T(8,128)(2,1)}), bf16[8,128,160]{1,2,0:T(8,128)(2,1)S(1)}, u32[]{:S(2)}, u32[]{:S(2)}) %all-to-all-start.6) | async-done | bytes 327712 | tf_op jit(solution)/shard_map/all_to_all | solution.py:455
  324.3 13.5 %reduce-scatter.4.cloned.1.call-done = bf16[128,2048]{1,0:T(8,128)(2,1)} async-done(((bf16[1024,2048]{1,0:T(8,128)(2,1)}), bf16[128,2048]{1,0:T(8,128)(2,1)}) %reduce-scatter.4.cloned.1.call-update) | async-done | bytes 524304 | tf_op jit(solution)/shard_map/reduce_scatter | solution.py:568
  350.6 7.4 %fusion.7 = bf16[1024,2048]{1,0:T(8,128)(2,1)S(1)} fusion(bf16[2048,512]{1,0:T(8,128)(2,1)} %constant_dynamic-update-slice_fusion.4, bf16[2048,512]{1,0:T(8,128)(2,1)} %constant_dynamic-update-slice_fusion.16, bf16[1024,512]{1,0:T(8,128)(2,1)} %copy-done.29, bf16[1024,512]{1,0:T(8,128)(2,1)} %copy-done.28), kind=kOutput, calls=%fused_computation.17 | convolution fusion | flops 4309647360 | bytes 10485760 | tf_op jit(solution)/shard_map/dot_general | solution.py:459
  364.4 6.1 %convolution_convert_fusion.1 = bf16[512,2048]{1,0:T(8,128)(2,1)} fusion(bf16[1024,512]{1,0:T(8,128)(2,1)S(1)} %copy-done.27, bf16[1024,2048]{1,0:T(8,128)(2,1)} %select_dynamic-update-slice_fusion, pred[1024]{0:T(1024)(128)(4,1)S(1)} %copy-done.44), kind=kOutput, calls=%fused_computation.23 | convolution fusion | flops 2150629376 | bytes 7341056 | tf_op jit(solution)/shard_map/dot_general | solution.py:459
  383.9 7.2 %collective-permute-done.34 = bf16[512,512]{1,0:T(8,128)(2,1)S(1)} collective-permute-done((bf16[512,512]{1,0:T(8,128)(2,1)S(1)}, bf16[512,512]{1,0:T(8,128)(2,1)S(1)}, u32[]{:S(2)}, u32[]{:S(2)}) %collective-permute-start.34) | collective-permute-done | bytes 524320 | tf_op jit(solution)/shard_map/ppermute | solution.py:309
  402.2 17.0 %collective-permute-start.30 = (bf16[128,2048]{1,0:T(8,128)(2,1)S(1)}, bf16[128,2048]{1,0:T(8,128)(2,1)S(1)}, u32[]{:S(2)}, u32[]{:S(2)}) collective-permute-start(bf16[128,2048]{1,0:T(8,128)(2,1)S(1)} %add_convert_fusion.4), channel_id=1, source_target_pairs={{0,2},{1,3},{2,4},{3,5},{8,10},{9,11},{10,12},{11,13},{16,18},{17,... | collective-permute-start | bytes 1572872 | tf_op jit(solution)/shard_map/ppermute | solution.py:342
  422.2 6.7 %collective-permute-done.30 = bf16[128,2048]{1,0:T(8,128)(2,1)S(1)} collective-permute-done((bf16[128,2048]{1,0:T(8,128)(2,1)S(1)}, bf16[128,2048]{1,0:T(8,128)(2,1)S(1)}, u32[]{:S(2)}, u32[]{:S(2)}) %collective-permute-start.30) | collective-permute-done | bytes 524320 | tf_op jit(solution)/shard_map/ppermute | solution.py:342
  432.2 8.9 %collective-permute-start.36 = (bf16[128,2048]{1,0:T(8,128)(2,1)}, bf16[128,2048]{1,0:T(8,128)(2,1)}, u32[]{:S(2)}, u32[]{:S(2)}) collective-permute-start(bf16[128,2048]{1,0:T(8,128)(2,1)} %get-tuple-element.107), channel_id=1, source_target_pairs={{0,2},{1,3},{2,4},{3,5},{4,6},{5,7},{8,10},{9,11},{10,12},{11,13},... | collective-permute-start | bytes 1572872 | tf_op jit(solution)/shard_map/ppermute | solution.py:342
  (283 shorter events, 211.7 us)
Async XLA Ops:
  7.2 151.6 %all-gather.3.cloned.1.call-start = ((), (), s32[]{:S(2)}) async-start(), calls=%async_computation.14 | async-start | bytes 4718592 | tf_op jit(solution)/shard_map/all_gather | solution.py:531
  16.9 28.9 %collective-permute-start.20 = (bf16[128,2048]{1,0:T(8,128)(2,1)}, bf16[128,2048]{1,0:T(8,128)(2,1)}, u32[]{:S(2)}, u32[]{:S(2)}) collective-permute-start(bf16[128,2048]{1,0:T(8,128)(2,1)} %param.24), channel_id=1, source_target_pairs={{0,16},{8,24},{16,0},{24,8},{1,17},{9,25},{17,1},{25,9},{2,18},{10... | collective-permute-start | bytes 1572872 | tf_op jit(solution)/shard_map/ppermute | solution.py:309
  17.0 30.3 %collective-permute-start.19 = (bf16[128,2048]{1,0:T(8,128)(2,1)}, bf16[128,2048]{1,0:T(8,128)(2,1)}, u32[]{:S(2)}, u32[]{:S(2)}) collective-permute-start(bf16[128,2048]{1,0:T(8,128)(2,1)} %param.24), channel_id=1, source_target_pairs={{0,8},{8,0},{16,24},{24,16},{1,9},{9,1},{17,25},{25,17},{2,10},{10... | collective-permute-start | bytes 1572872 | tf_op jit(solution)/shard_map/ppermute | solution.py:302
  25.3 47.4 %all-to-all-start = ((bf16[8,64,512]{2,1,0:T(8,128)(2,1)}), bf16[8,64,512]{2,1,0:T(8,128)(2,1)S(1)}, u32[]{:S(2)}, u32[]{:S(2)}) async-start(bf16[8,64,512]{2,1,0:T(8,128)(2,1)} %squeeze.29), calls=%async_computation | async-start | bytes 1048576 | tf_op jit(solution)/shard_map/all_to_all | solution.py:493
  37.3 27.3 %collective-permute-start.6 = (bf16[128,2048]{1,0:T(8,128)(2,1)S(1)}, bf16[128,2048]{1,0:T(8,128)(2,1)S(1)}, u32[]{:S(2)}, u32[]{:S(2)}) collective-permute-start(bf16[128,2048]{1,0:T(8,128)(2,1)S(1)} %bitcast.110), channel_id=1, source_target_pairs={{0,1},{1,0},{2,3},{3,2},{4,5},{5,4},{6,7},{7,6},{8,9},{9,8},{10,11... | collective-permute-start | bytes 1572872 | tf_op jit(solution)/shard_map/ppermute | solution.py:347
  44.4 50.1 %collective-permute-start.11 = (bf16[128,2048]{1,0:T(8,128)(2,1)}, bf16[128,2048]{1,0:T(8,128)(2,1)}, u32[]{:S(2)}, u32[]{:S(2)}) collective-permute-start(bf16[128,2048]{1,0:T(8,128)(2,1)} %collective-permute-done.7), channel_id=1, source_target_pairs={{2,4},{3,5},{4,6},{5,7},{10,12},{11,13},{12,14},{13,15},{18,20},{1... | collective-permute-start | bytes 1572872 | tf_op jit(solution)/shard_map/ppermute | solution.py:342
  45.8 36.3 %collective-permute-start.9 = (bf16[128,2048]{1,0:T(8,128)(2,1)}, bf16[128,2048]{1,0:T(8,128)(2,1)}, u32[]{:S(2)}, u32[]{:S(2)}) collective-permute-start(bf16[128,2048]{1,0:T(8,128)(2,1)} %collective-permute-done.7), channel_id=1, source_target_pairs={{2,3},{3,2},{4,5},{5,4},{6,7},{7,6},{10,11},{11,10},{12,13},{13,12... | collective-permute-start | bytes 1572872 | tf_op jit(solution)/shard_map/ppermute | solution.py:347
  47.3 126.4 %collective-permute-start.21 = (bf16[128,2048]{1,0:T(8,128)(2,1)}, bf16[128,2048]{1,0:T(8,128)(2,1)}, u32[]{:S(2)}, u32[]{:S(2)}) collective-permute-start(bf16[128,2048]{1,0:T(8,128)(2,1)} %collective-permute-done.20), channel_id=1, source_target_pairs={{0,8},{8,0},{16,24},{24,16},{1,9},{9,1},{17,25},{25,17},{2,10},{10... | collective-permute-start | bytes 1572872 | tf_op jit(solution)/shard_map/ppermute | solution.py:302
  61.2 33.5 %collective-permute-start.12 = (bf16[128,2048]{1,0:T(8,128)(2,1)}, bf16[128,2048]{1,0:T(8,128)(2,1)}, u32[]{:S(2)}, u32[]{:S(2)}) collective-permute-start(bf16[128,2048]{1,0:T(8,128)(2,1)} %collective-permute-done.8), channel_id=1, source_target_pairs={{2,0},{3,1},{4,2},{5,3},{10,8},{11,9},{12,10},{13,11},{18,16},{19,... | collective-permute-start | bytes 1572872 | tf_op jit(solution)/shard_map/ppermute | solution.py:342
  64.6 27.9 %collective-permute-start.10 = (bf16[128,2048]{1,0:T(8,128)(2,1)}, bf16[128,2048]{1,0:T(8,128)(2,1)}, u32[]{:S(2)}, u32[]{:S(2)}) collective-permute-start(bf16[128,2048]{1,0:T(8,128)(2,1)} %collective-permute-done.8), channel_id=1, source_target_pairs={{0,1},{1,0},{2,3},{3,2},{4,5},{5,4},{8,9},{9,8},{10,11},{11,10},{1... | collective-permute-start | bytes 1572872 | tf_op jit(solution)/shard_map/ppermute | solution.py:347
  74.1 27.8 %all-to-all-start.1 = ((bf16[8,2,128]{2,1,0:T(2,128)(2,1)}), bf16[8,2,128]{2,1,0:T(2,128)(2,1)}, u32[]{:S(2)}, u32[]{:S(2)}) async-start(bf16[8,2,128]{2,1,0:T(2,128)(2,1)} %reshape.120), calls=%async_computation.1 | async-start | bytes 8192 | tf_op jit(solution)/shard_map/all_to_all | solution.py:455
  82.1 40.1 %collective-permute-start.4 = (bf16[512,512]{1,0:T(8,128)(2,1)S(1)}, bf16[512,512]{1,0:T(8,128)(2,1)S(1)}, u32[]{:S(2)}, u32[]{:S(2)}) collective-permute-start(bf16[512,512]{1,0:T(8,128)(2,1)S(1)} %bitcast.113), channel_id=1, source_target_pairs={{0,16},{8,24},{16,0},{24,8},{1,17},{9,25},{17,1},{25,9},{2,18},{10... | collective-permute-start | bytes 1572872 | tf_op jit(solution)/shard_map/ppermute | solution.py:309
  92.5 29.8 %collective-permute-start.3 = (bf16[512,512]{1,0:T(8,128)(2,1)S(1)}, bf16[512,512]{1,0:T(8,128)(2,1)}, u32[]{:S(2)}, u32[]{:S(2)}) collective-permute-start(bf16[512,512]{1,0:T(8,128)(2,1)S(1)} %bitcast.114), channel_id=1, source_target_pairs={{0,8},{8,0},{16,24},{24,16},{1,9},{9,1},{17,25},{25,17},{2,10},{10... | collective-permute-start | bytes 1572872 | tf_op jit(solution)/shard_map/ppermute | solution.py:302
  96.9 44.0 %collective-permute-start.13 = (bf16[128,2048]{1,0:T(8,128)(2,1)}, bf16[128,2048]{1,0:T(8,128)(2,1)}, u32[]{:S(2)}, u32[]{:S(2)}) collective-permute-start(bf16[128,2048]{1,0:T(8,128)(2,1)} %get-tuple-element.106), channel_id=1, source_target_pairs={{0,1},{1,0},{2,3},{3,2},{4,5},{5,4},{6,7},{7,6},{8,9},{9,8},{10,11... | collective-permute-start | bytes 1572872 | tf_op jit(solution)/shard_map/ppermute | solution.py:347
  98.3 39.1 %collective-permute-start.14 = (bf16[128,2048]{1,0:T(8,128)(2,1)}, bf16[128,2048]{1,0:T(8,128)(2,1)}, u32[]{:S(2)}, u32[]{:S(2)}) collective-permute-start(bf16[128,2048]{1,0:T(8,128)(2,1)} %get-tuple-element.106), channel_id=1, source_target_pairs={{4,6},{5,7},{2,0},{3,1},{12,14},{13,15},{10,8},{11,9},{20,22},{21,... | collective-permute-start | bytes 1572872 | tf_op jit(solution)/shard_map/ppermute | solution.py:342
  104.1 40.8 %all-to-all-start.4 = ((bf16[8,64,512]{2,1,0:T(8,128)(2,1)}), bf16[8,64,512]{2,1,0:T(8,128)(2,1)}, u32[]{:S(2)}, u32[]{:S(2)}) async-start(bf16[8,64,512]{2,1,0:T(8,128)(2,1)} %squeeze.28), calls=%async_computation.4 | async-start | bytes 1048576 | tf_op jit(solution)/shard_map/all_to_all | solution.py:520
  146.5 31.8 %collective-permute-start.16 = (bf16[512,512]{1,0:T(8,128)(2,1)}, bf16[512,512]{1,0:T(8,128)(2,1)}, u32[]{:S(2)}, u32[]{:S(2)}) collective-permute-start(bf16[512,512]{1,0:T(8,128)(2,1)} %bitcast.20), channel_id=1, source_target_pairs={{0,8},{8,0},{16,24},{24,16},{1,9},{9,1},{17,25},{25,17},{2,10},{10... | collective-permute-start | bytes 1572872 | tf_op jit(solution)/shard_map/ppermute | solution.py:302
  201.2 136.6 %reduce-scatter.4.cloned.1.call-start = ((), (), s32[]{:S(2)}) async-start(), calls=%async_computation.11 | async-start | bytes 4718592 | tf_op jit(solution)/shard_map/reduce_scatter | solution.py:568
  253.6 41.6 %collective-permute-start.22 = (bf16[512,512]{1,0:T(8,128)(2,1)}, bf16[512,512]{1,0:T(8,128)(2,1)}, u32[]{:S(2)}, u32[]{:S(2)}) collective-permute-start(bf16[512,512]{1,0:T(8,128)(2,1)} %get-tuple-element.118), channel_id=1, source_target_pairs={{0,8},{8,0},{16,24},{24,16},{1,9},{9,1},{17,25},{25,17},{2,10},{10... | collective-permute-start | bytes 1572872 | tf_op jit(solution)/shard_map/ppermute | solution.py:302
  310.1 132.3 %reduce-scatter.6.cloned.1.call-start = ((), (), s32[]{:S(2)}) async-start(), calls=%async_computation.12 | async-start | bytes 798720 | tf_op jit(solution)/shard_map/reduce_scatter | solution.py:632
  350.6 111.3 %reduce-scatter.8.cloned.1.call-start = ((), (), s32[]{:S(2)}) async-start(), calls=%async_computation.13 | async-start | bytes 2621440 | tf_op jit(solution)/shard_map/reduce_scatter | solution.py:618
  370.5 29.2 %collective-permute-start.29 = (bf16[128,2048]{1,0:T(8,128)(2,1)}, bf16[128,2048]{1,0:T(8,128)(2,1)}, u32[]{:S(2)}, u32[]{:S(2)}) collective-permute-start(bf16[128,2048]{1,0:T(8,128)(2,1)} %get-tuple-element.111), channel_id=1, source_target_pairs={{2,3},{3,2},{4,5},{5,4},{6,7},{7,6},{10,11},{11,10},{12,13},{13,12... | collective-permute-start | bytes 1572872 | tf_op jit(solution)/shard_map/ppermute | solution.py:347
  372.0 27.7 %collective-permute-start.28 = (bf16[128,2048]{1,0:T(8,128)(2,1)}, bf16[128,2048]{1,0:T(8,128)(2,1)}, u32[]{:S(2)}, u32[]{:S(2)}) collective-permute-start(bf16[128,2048]{1,0:T(8,128)(2,1)} %get-tuple-element.112), channel_id=1, source_target_pairs={{0,1},{1,0},{2,3},{3,2},{4,5},{5,4},{8,9},{9,8},{10,11},{11,10},{1... | collective-permute-start | bytes 1572872 | tf_op jit(solution)/shard_map/ppermute | solution.py:347
  393.6 55.7 %all-to-all-start.7 = ((bf16[8,64,1024]{2,1,0:T(8,128)(2,1)}), bf16[8,64,1024]{2,1,0:T(8,128)(2,1)}, u32[]{:S(2)}, u32[]{:S(2)}) async-start(bf16[8,64,1024]{2,1,0:T(8,128)(2,1)} %pad_maximum_fusion), calls=%async_computation.9 | async-start | bytes 2097152 | tf_op jit(solution)/shard_map/all_to_all | solution.py:624
  (71 other events, 1208.0 us)
Sparse Core Ops, SparseCore 0:
  10.1 115.0 all-gather.2
  243.2 94.6 reduce-scatter.3
  350.7 21.1 reduce-scatter.5
  374.5 31.3 reduce-scatter.7
where the time goes:
time: 477 us; the launch traced here: 471 us
  starting transfers between devices  136 us (29%)
  waiting for transfers between devices  92.3 us (19%)
  local copies, waits for them, and re-layouts  79 us (17%)
  other arithmetic  50.7 us (11%)
  matrix products  49.6 us (10%)
  Pallas kernels  47.4 us (10%)
  between operations  15.7 us (3%)
    dot_general x14, matrix products, matmul(): return lax.dot_general(a, b, dims, preferred_element_type=f32)  49.6 us
    ppermute x10, starting transfers between devices, hop(): return lax.ppermute(value, axis, pairs)  40.5 us
    ppermute x10, waiting for transfers between devices, hop(): return lax.ppermute(value, axis, pairs)  33.7 us
    pallas_call x1, Pallas kernels, scan_backward(): pl.pallas_call(functools.partial(backward_body, tiles, step), grid=(block...  31 us
    all_to_all x3, starting transfers between devices, shared(): return lax.all_to_all(wide, axis, 0, 0)  27.2 us
    ppermute x10, starting transfers between devices, swap_at(): return lax.ppermute(value, axis, pairs)  22.7 us
    dynamic_update_slice x16, local copies, waits for them, and re-layouts, gathered(): whole = lax.dynamic_update_slice_in_dim(whole, piece, place * size, dim)  20 us
    all_to_all x1, starting transfers between devices, on_device(): gate_columns = lax.all_to_all(gate_columns, 'seq', 0, 0)  18.1 us
  transfers between devices with their start and end apart: 50, of which 17 were waited for; matrix products, arithmetic and copies ran while one was open for 31% of the time, Pallas kernels for 7%

commit v1 on v0

--- a/solution.py
+++ b/solution.py
@@ -350,9 +350,9 @@
 UP, DOWN = [(0, 1), (1, 2), (2, 3)], [(1, 0), (2, 1), (3, 2)]
 
 
-def line_gathered(own, axis):
+def line_gathered(own, axis, held):
     if lax.axis_size(axis) != 8:
-        return lax.all_gather(own, axis, axis=0, tiled=True)
+        return lax.all_gather(own, axis, axis=0, tiled=True), held
     place = lax.axis_index(axis)
     z, x = place // 2, place % 2
     rows = own.shape[0]
@@ -368,7 +368,9 @@
         return put(whole, jnp.where(edge, piece, held), far, side)
 
     whole = jnp.zeros((8 * rows,) + own.shape[1:], own.dtype)
-    up, down, other = hop(own, axis, UP), hop(own, axis, DOWN), swap_at(own, axis, range(4))
+    up, down, other, held = together(
+        (hop(own, axis, UP), hop(own, axis, DOWN), swap_at(own, axis, range(4)), held)
+    )
     up_two, down_two = hop(up, axis, UP[1:]), hop(down, axis, DOWN[:2])
     other_up, other_down = swap_at(up, axis, (1, 2, 3)), swap_at(down, axis, (0, 1, 2))
     whole = put(put(whole, own, z, x), other, z, 1 - x)
@@ -380,7 +382,7 @@
     whole = put(whole, two, across, x)
     other_three = swap_at(three, axis, (0, 3))
     whole = put(whole, other_two, across, 1 - x)
-    return put_far(put_far(whole, three, x), other_three, 1 - x)
+    return put_far(put_far(whole, three, x), other_three, 1 - x), held
 
 
 def line_summed(part_of, axis):
@@ -521,7 +523,6 @@
     gain = gain.transpose(1, 0, 2).reshape(model).astype(f32)
 
     input_weight = gathered(columns.reshape(seq * in_rows, width), "batch")
-    output_weight = gathered(out_proj, "batch")
 
     def normed(rows):
         rows = rows.astype(f32)
@@ -531,7 +532,8 @@
     stream = lax.all_gather(tokens[0], "seq", axis=0, tiled=True)
     gate_weight = gathered(gate_columns.reshape(seq * in_rows, width), "batch")
     normalized = normed(stream)
-    upstream = line_gathered(cotangent[0], "seq")
+    upstream, out_proj = line_gathered(cotangent[0], "seq", out_proj)
+    output_weight = gathered(out_proj, "batch")
 
     valid = (jnp.arange(length, dtype=jnp.int32) < lengths[0])[:, None]
     inner = matmul(normalized, input_weight).astype(bf16)
@@ -568,7 +570,6 @@
     branch = lax.psum_scatter(branch, "seq", scatter_dimension=0, tiled=True)
     own_valid = lax.dynamic_slice_in_dim(valid, place * span, span, 0)
     own_stream = tokens[0].astype(f32)
-    block_out = jnp.where(own_valid, own_stream + branch.astype(f32), 0.0)
 
     d_mixed = d_gated * gate * gate_sig
     d_gate = d_gated * mixed * gate_sig * (1.0 + gate * (1.0 - gate_sig))
@@ -587,7 +588,7 @@
     grad_gate = scattered_sum(
         rows_of(matmul(normalized, d_gate_low, TN).astype(bf16), model // batch), "batch"
     )
-    d_select, branch, grad_gate = together((d_select, branch, grad_gate))
+    d_select, grad_gate = together((d_select, grad_gate))
     grad_x_proj = matmul(d_select, active, TN)
     d_active = d_active + d_mixed * skip_gain + matmul(d_select, select_weight)
     conv_sig = jax.nn.sigmoid(conv_out)
@@ -607,23 +608,30 @@
         d_inner = d_inner + conv_taps[tap] * extended[offset : offset + length].astype(f32)
     d_inner = d_inner.astype(bf16)
     grad_inner = matmul(normalized, d_inner, TN).astype(bf16)
-    d_inner, grad_inner = together((d_inner, grad_inner))
+    d_inner, grad_inner, branch = together((d_inner, grad_inner, branch))
     d_normalized = matmul(
         jnp.concatenate([d_inner, d_gate_low], axis=1),
         jnp.concatenate([input_weight, gate_weight], axis=1),
         NT,
     ).astype(bf16)
     grad_inner = scattered_sum(rows_of(grad_inner, model // batch), "batch")
-    d_normalized, gated = together((d_normalized, gated))
+    grad_gate = grad_gate.astype(bf16).reshape(seq, in_rows, width)
+    grad_gate = lax.all_to_all(grad_gate, "seq", 0, 0)
+    d_normalized, gated, grad_gate = together((d_normalized, gated, grad_gate))
     grad_output = lax.psum_scatter(
         matmul(gated, upstream, TN).astype(bf16), "batch", scatter_dimension=0, tiled=True
     ).astype(f32)
     d_normalized, *last_terms = line_summed(rows_of(d_normalized, span), "seq")
 
-    both = jnp.concatenate([grad_inner, grad_gate], axis=1).astype(bf16)
-    both = lax.all_to_all(both.reshape(seq, in_rows, 2 * width), "seq", 0, 0)
-    both = both.reshape(seq, in_rows, 2, batch, own).transpose(1, 2, 3, 0, 4)
-    grad_input = both.reshape(in_rows, 2 * batch * seq * own).astype(f32)
+    block_out = jnp.where(own_valid, own_stream + branch.astype(f32), 0.0)
+
+    def columns_of(part):
+        part = part.reshape(seq, in_rows, batch, own).transpose(1, 2, 0, 3)
+        return part.reshape(in_rows, batch * seq * own).astype(f32)
+
+    grad_inner = grad_inner.astype(bf16).reshape(seq, in_rows, width)
+    grad_inner = lax.all_to_all(grad_inner, "seq", 0, 0)
+    grad_input = jnp.concatenate([columns_of(grad_inner), columns_of(grad_gate)], axis=1)
 
     small_grads = jnp.concatenate(
         [grad_dt_proj, grad_x_proj, grad_log, grad_conv, grad_conv_bias, grad_dt_bias, grad_skip],
@@ -639,11 +647,11 @@
     grad_gain = jnp.sum(grad_input * in_proj.astype(f32), axis=1) / norm_gain.astype(f32)
     (
         d_normalized, g_dt_proj, g_x_proj, g_log, g_conv, g_conv_bias, g_dt_bias, g_skip,
-        grad_input, grad_gain,
+        grad_input, grad_gain, grad_output,
     ) = together(
         (
             d_normalized, g_dt_proj, g_x_proj, g_log, g_conv, g_conv_bias, g_dt_bias, g_skip,
-            grad_input, grad_gain,
+            grad_input, grad_gain, grad_output,
         )
     )
     for term in last_terms:

time: 477 us -> 457 us (0.958)
  starting transfers between devices: 136 us -> 106 us
  waiting for transfers between devices: 92.3 us -> 115 us
  local copies, waits for them, and re-layouts: 79 us -> 68.9 us
    all_to_all x3, waiting for transfers between devices: 10.4 us -> 40.6 us  [shared(): return lax.all_to_all(wide, axis, 0, 0)]
    ppermute x10, starting transfers between devices: 40.5 us -> 21.9 us  [hop(): return lax.ppermute(value, axis, pairs)]
    ppermute x10, waiting for transfers between devices: 33.7 us -> 16.2 us  [hop(): return lax.ppermute(value, axis, pairs)]
    ppermute x10, waiting for transfers between devices: 14.8 us -> 28.9 us  [swap_at(): return lax.ppermute(value, axis, pairs)]
    all_to_all x1, starting transfers between devices: 18.1 us -> 4.16 us  [on_device(): gate_columns = lax.all_to_all(gate_columns, 'seq', 0, 0)]
    reduce_scatter x1, waiting for transfers between devices: 13.5 us -> 1.3 us  [on_device(): branch = lax.psum_scatter(branch, 'seq', scatter_dimension=0, tiled=True)]
    ppermute x6, waiting for transfers between devices: 11.6 us -> 17.2 us  [outer_shift(): return lax.ppermute(value, axis, pairs)]
    dynamic_update_slice x7 -> x6, local copies, waits for them, and re-layouts: 11.2 us -> 8.25 us  [put(): lax.dynamic_update_slice_in_dim(whole, piece, (spot * 2 + side) * rows, 0)]
  transfers between devices with their start and end apart: 50 -> 51, of which waited for: 17 -> 18; matrix products, arithmetic and copies ran while one was open for 31% -> 33% of each run, Pallas kernels for 7% -> 7%
where the time goes in v1:
time: 457 us; the launch traced here: 451 us
  waiting for transfers between devices  115 us (25%)
  starting transfers between devices  106 us (23%)
  local copies, waits for them, and re-layouts  68.9 us (15%)
  matrix products  52 us (11%)
  Pallas kernels  47.4 us (10%)
  other arithmetic  46.8 us (10%)
  between operations  15.7 us (3%)
    dot_general x14, matrix products, matmul(): return lax.dot_general(a, b, dims, preferred_element_type=f32)  52 us
    all_to_all x3, waiting for transfers between devices, shared(): return lax.all_to_all(wide, axis, 0, 0)  40.6 us
    pallas_call x1, Pallas kernels, scan_backward(): pl.pallas_call(functools.partial(backward_body, tiles, step), grid=(block...  31 us
    ppermute x10, waiting for transfers between devices, swap_at(): return lax.ppermute(value, axis, pairs)  28.9 us
    all_to_all x3, starting transfers between devices, shared(): return lax.all_to_all(wide, axis, 0, 0)  28.6 us
    ppermute x10, starting transfers between devices, hop(): return lax.ppermute(value, axis, pairs)  21.9 us
    ppermute x10, starting transfers between devices, swap_at(): return lax.ppermute(value, axis, pairs)  18.7 us
    ppermute x6, waiting for transfers between devices, outer_shift(): return lax.ppermute(value, axis, pairs)  17.2 us
  transfers between devices with their start and end apart: 51, of which 18 were waited for; matrix products, arithmetic and copies ran while one was open for 33% of the time, Pallas kernels for 7%

profile of v1, /device:TPU:0, one launch (start us, length us, event | category | flops | bytes accessed | tf_op | source)
XLA Modules:
  0.0 451.5 jit_solution(3512044184288887621)
XLA Ops:
  25.2 5.9 %all-to-all-start = ((bf16[8,64,512]{2,1,0:T(8,128)(2,1)}), bf16[8,64,512]{2,1,0:T(8,128)(2,1)S(1)}, u32[]{:S(2)}, u32[]{:S(2)}) async-start(bf16[8,64,512]{2,1,0:T(8,128)(2,1)} %squeeze.29), calls=%async_computation | async-start | bytes 1048576 | tf_op jit(solution)/shard_map/all_to_all | solution.py:495
  39.6 14.2 %collective-permute-done.7 = bf16[128,2048]{1,0:T(8,128)(2,1)} collective-permute-done((bf16[128,2048]{1,0:T(8,128)(2,1)}, bf16[128,2048]{1,0:T(8,128)(2,1)}, u32[]{:S(2)}, u32[]{:S(2)}) %collective-permute-start.7) | collective-permute-done | bytes 524320 | tf_op jit(solution)/shard_map/ppermute | solution.py:342
  67.7 8.5 %all-to-all-start.1 = ((bf16[8,2,128]{2,1,0:T(2,128)(2,1)}), bf16[8,2,128]{2,1,0:T(2,128)(2,1)}, u32[]{:S(2)}, u32[]{:S(2)}) async-start(bf16[8,2,128]{2,1,0:T(2,128)(2,1)} %reshape.127), calls=%async_computation.1 | async-start | bytes 8192 | tf_op jit(solution)/shard_map/all_to_all | solution.py:457
  78.5 29.6 %all-to-all-done.1 = bf16[8,2,128]{2,1,0:T(2,128)(2,1)} async-done(((bf16[8,2,128]{2,1,0:T(2,128)(2,1)}), bf16[8,2,128]{2,1,0:T(2,128)(2,1)}, u32[]{:S(2)}, u32[]{:S(2)}) %all-to-all-start.1) | async-done | bytes 4128 | tf_op jit(solution)/shard_map/all_to_all | solution.py:457
  127.3 7.9 %collective-permute-done.4 = bf16[512,512]{1,0:T(8,128)(2,1)} collective-permute-done((bf16[512,512]{1,0:T(8,128)(2,1)S(1)}, bf16[512,512]{1,0:T(8,128)(2,1)}, u32[]{:S(2)}, u32[]{:S(2)}) %collective-permute-start.4) | collective-permute-done | bytes 524320 | tf_op jit(solution)/shard_map/ppermute | solution.py:309
  146.4 8.7 %collective-permute-done.15 = bf16[128,2048]{1,0:T(8,128)(2,1)S(1)} collective-permute-done((bf16[128,2048]{1,0:T(8,128)(2,1)}, bf16[128,2048]{1,0:T(8,128)(2,1)S(1)}, u32[]{:S(2)}, u32[]{:S(2)}) %collective-permute-start.15) | collective-permute-done | bytes 524320 | tf_op jit(solution)/shard_map/ppermute | solution.py:347
  171.0 5.7 %all-to-all-start.2 = ((bf16[8,128,160]{1,2,0:T(8,128)(2,1)}), bf16[8,128,160]{1,2,0:T(8,128)(2,1)S(1)}, u32[]{:S(2)}, u32[]{:S(2)}) async-start(bf16[8,128,160]{1,2,0:T(8,128)(2,1)} %copy_bitcast_fusion.4), calls=%async_computation.2 | async-start | bytes 655360 | tf_op jit(solution)/shard_map/all_to_all | solution.py:446
  188.5 16.5 %all-to-all-start.3 = ((bf16[8,128,192]{1,2,0:T(8,128)(2,1)}), bf16[8,128,192]{1,2,0:T(8,128)(2,1)}, u32[]{:S(2)}, u32[]{:S(2)}) async-start(bf16[8,128,192]{1,2,0:T(8,128)(2,1)} %broadcast_in_dim.96), calls=%async_computation.3 | async-start | bytes 786432 | tf_op jit(solution)/shard_map/all_to_all | solution.py:457
  205.1 6.0 %fusion.34 = f32[1024,512]{1,0:T(8,128)} fusion(bf16[512,2048]{1,0:T(8,128)(2,1)S(1)} %constant_dynamic-update-slice_fusion, bf16[1024,2048]{1,0:T(8,128)(2,1)} %select_dynamic-update-slice_fusion, pred[1024]{0:T(1024)(128)(4,1)} %iota_compare_fusion), kind=kOutput, calls=%fused_computation.65 | convolution fusion | flops 2149580800 | bytes 8389632 | tf_op jit(solution)/shard_map/dot_general | solution.py:461
  211.2 5.0 %convolution_convert_fusion.4 = bf16[1024,512]{1,0:T(8,128)(2,1)} fusion(bf16[2048,512]{1,0:T(8,128)(2,1)} %constant_dynamic-update-slice_fusion.4, bf16[1,1024,2048]{2,1,0:T(8,128)(2,1)S(1)} %copy-done.9, f32[2048]{0:T(1024)S(1)} %reshape.120, f32[1024]{0:T(1024)S(1)} %copy-done.40), kind=kOutput, calls=%fused_computation.66 | convolution fusion | flops 2156396544 | bytes 7352320 | tf_op jit(solution)/shard_map/dot_general | solution.py:461
  222.1 16.4 %scan_forward.1 = (f32[1024,512]{1,0:T(8,128)S(1)}, bf16[16384,512]{1,0:T(8,128)(2,1)}) custom-call(f32[1024,512]{1,0:T(8,128)S(1)} %get-tuple-element.152.delta, bf16[1024,512]{1,0:T(8,128)(2,1)S(1)} %multiply_convert_fusion.1.active, bf16[1024,192]{1,0:T(8,128)(2,1)S(1)} %bitcast.105, f32[16,512]{1,0:T(8,128)S(1)} %get-tuple-element.140.rate), custom_call_target="tpu_custom_call" | custom-call | flops 67108864 | bytes 22020096 | tf_op jit(solution)/shard_map/scan_forward/pallas_call | solution.py:90
  246.1 6.7 %fusion.15 = (f32[512]{0:T(512)}, f32[1024,512]{1,0:T(8,128)}, bf16[1024,512]{1,0:T(8,128)(2,1)S(1)}) fusion(f32[1024,512]{1,0:T(8,128)} %fusion.34, bf16[1024,512]{1,0:T(8,128)(2,1)} %convolution_convert_fusion.4, f32[1024,512]{1,0:T(8,128)S(1)} %get-tuple-element.71, f32[512]{0:T(512)} %bitcast.151, bf16[1024,512]{1,0:T(8,128)(2,1)} %copy-done.4, ...), kind=kLoop, calls=%fused_computation.37 | loop fusion | flops 18349568 | bytes 9451520 | tf_op jit(solution)/shard_map/reduce_sum | solution.py:576
  257.2 31.0 %scan_backward.1 = (f32[1024,512]{1,0:T(8,128)S(1)}, f32[1024,512]{1,0:T(8,128)}, f32[1024,32]{1,0:T(8,128)S(1)}, f32[16,512]{1,0:T(8,128)S(1)}) custom-call(f32[1024,512]{1,0:T(8,128)} %copy-done.3, bf16[1024,512]{1,0:T(8,128)(2,1)S(1)} %multiply_convert_fusion.1.active, f32[1024,512]{1,0:T(8,128)} %get-tuple-element.114.d_mixed, ...), custom_call_target="tpu_custom_call" | custom-call | flops 167772160 | bytes 27262976 | tf_op jit(solution)/shard_map/scan_backward/pallas_call | solution.py:251
  292.6 5.3 %all-to-all-start.5 = ((bf16[8,128,160]{1,2,0:T(8,128)(2,1)}), bf16[8,128,160]{1,2,0:T(8,128)(2,1)S(1)}, u32[]{:S(2)}, u32[]{:S(2)}) async-start(bf16[8,128,160]{1,2,0:T(8,128)(2,1)} %pad_maximum_fusion), calls=%async_computation.5 | async-start | bytes 655360 | tf_op jit(solution)/shard_map/all_to_all | solution.py:446
  300.4 7.9 %all-to-all-done.5 = bf16[8,128,160]{1,2,0:T(8,128)(2,1)S(1)} async-done(((bf16[8,128,160]{1,2,0:T(8,128)(2,1)}), bf16[8,128,160]{1,2,0:T(8,128)(2,1)S(1)}, u32[]{:S(2)}, u32[]{:S(2)}) %all-to-all-start.5) | async-done | bytes 327712 | tf_op jit(solution)/shard_map/all_to_all | solution.py:446
  317.2 10.4 %all-to-all-done.6 = bf16[8,128,160]{1,2,0:T(8,128)(2,1)S(1)} async-done(((bf16[8,128,160]{1,2,0:T(8,128)(2,1)}), bf16[8,128,160]{1,2,0:T(8,128)(2,1)S(1)}, u32[]{:S(2)}, u32[]{:S(2)}) %all-to-all-start.6) | async-done | bytes 327712 | tf_op jit(solution)/shard_map/all_to_all | solution.py:457
  327.6 4.8 %all-to-all-start.7 = ((bf16[8,64,512]{2,1,0:T(8,128)(2,1)}), bf16[8,64,512]{2,1,0:T(8,128)(2,1)S(1)}, u32[]{:S(2)}, u32[]{:S(2)}) async-start(bf16[8,64,512]{2,1,0:T(8,128)(2,1)} %bitcast.27), calls=%async_computation.8 | async-start | bytes 1048576 | tf_op jit(solution)/shard_map/all_to_all | solution.py:619
  342.5 5.2 %convolution_convert_fusion.2 = bf16[2048,512]{1,0:T(8,128)(2,1)S(1)} fusion(bf16[1024,512]{1,0:T(8,128)(2,1)} %get-tuple-element.81, bf16[1,1024,2048]{2,1,0:T(8,128)(2,1)} %all-gather.3.cloned.1.call-done, f32[2048]{0:T(1024)S(1)} %reshape.120, f32[1024]{0:T(1024)S(1)} %copy-done.42), kind=kOutput, calls=%fused_computation.24 | convolution fusion | flops 2156920832 | bytes 7352320 | tf_op jit(solution)/shard_map/dot_general | solution.py:461
  349.0 9.4 %fusion.7 = bf16[1024,2048]{1,0:T(8,128)(2,1)} fusion(bf16[2048,512]{1,0:T(8,128)(2,1)} %constant_dynamic-update-slice_fusion.4, bf16[2048,512]{1,0:T(8,128)(2,1)} %constant_dynamic-update-slice_fusion.16, bf16[1024,512]{1,0:T(8,128)(2,1)} %copy-done.24, bf16[1024,512]{1,0:T(8,128)(2,1)} %get-tuple-element.81), kind=kOutput, calls=%fused_computation.17 | convolution fusion | flops 4309647360 | bytes 10485760 | tf_op jit(solution)/shard_map/dot_general | solution.py:461
  369.9 6.0 %convolution_convert_fusion.1 = bf16[512,2048]{1,0:T(8,128)(2,1)} fusion(bf16[1024,512]{1,0:T(8,128)(2,1)S(1)} %copy-done.23, bf16[1024,2048]{1,0:T(8,128)(2,1)} %select_dynamic-update-slice_fusion, pred[1024]{0:T(1024)(128)(4,1)S(1)} %copy-done.44), kind=kOutput, calls=%fused_computation.23 | convolution fusion | flops 2150629376 | bytes 7341056 | tf_op jit(solution)/shard_map/dot_general | solution.py:461
  381.5 8.3 %collective-permute-done.27 = bf16[128,2048]{1,0:T(8,128)(2,1)} collective-permute-done((bf16[128,2048]{1,0:T(8,128)(2,1)}, bf16[128,2048]{1,0:T(8,128)(2,1)}, u32[]{:S(2)}, u32[]{:S(2)}) %collective-permute-start.27) | collective-permute-done | bytes 524320 | tf_op jit(solution)/shard_map/ppermute | solution.py:347
  390.8 9.4 %collective-permute-done.28 = bf16[128,2048]{1,0:T(8,128)(2,1)} collective-permute-done((bf16[128,2048]{1,0:T(8,128)(2,1)}, bf16[128,2048]{1,0:T(8,128)(2,1)}, u32[]{:S(2)}, u32[]{:S(2)}) %collective-permute-start.28) | collective-permute-done | bytes 524320 | tf_op jit(solution)/shard_map/ppermute | solution.py:347
  407.8 4.8 %collective-permute-done.34 = bf16[512,512]{1,0:T(8,128)(2,1)S(1)} collective-permute-done((bf16[512,512]{1,0:T(8,128)(2,1)S(1)}, bf16[512,512]{1,0:T(8,128)(2,1)S(1)}, u32[]{:S(2)}, u32[]{:S(2)}) %collective-permute-start.34) | collective-permute-done | bytes 524320 | tf_op jit(solution)/shard_map/ppermute | solution.py:309
  430.3 4.6 %collective-permute-start.36 = (bf16[128,2048]{1,0:T(8,128)(2,1)}, bf16[128,2048]{1,0:T(8,128)(2,1)S(1)}, u32[]{:S(2)}, u32[]{:S(2)}) collective-permute-start(bf16[128,2048]{1,0:T(8,128)(2,1)} %get-tuple-element.121), channel_id=1, source_target_pairs={{0,2},{1,3},{2,4},{3,5},{4,6},{5,7},{8,10},{9,11},{10,12},{11,13},... | collective-permute-start | bytes 1572872 | tf_op jit(solution)/shard_map/ppermute | solution.py:342
  (288 shorter events, 197.5 us)
Async XLA Ops:
  7.2 152.7 %all-gather.3.cloned.1.call-start = ((), (), s32[]{:S(2)}) async-start(), calls=%async_computation.15 | async-start | bytes 4718592 | tf_op jit(solution)/shard_map/all_gather | solution.py:532
  11.5 25.4 %collective-permute-start = (bf16[312,128]{1,0:T(8,128)(2,1)S(1)}, bf16[312,128]{1,0:T(8,128)(2,1)S(1)}, u32[]{:S(2)}, u32[]{:S(2)}) collective-permute-start(bf16[312,128]{1,0:T(8,128)(2,1)S(1)} %concatenate.30), channel_id=1, source_target_pairs={{0,8},{8,0},{16,24},{24,16},{1,9},{9,1},{17,25},{25,17},{2,10},{10... | collective-permute-start | bytes 239624 | tf_op jit(solution)/shard_map/ppermute | solution.py:302
  19.0 34.8 %collective-permute-start.7 = (bf16[128,2048]{1,0:T(8,128)(2,1)}, bf16[128,2048]{1,0:T(8,128)(2,1)}, u32[]{:S(2)}, u32[]{:S(2)}) collective-permute-start(bf16[128,2048]{1,0:T(8,128)(2,1)} %bitcast.116), channel_id=1, source_target_pairs={{2,0},{3,1},{4,2},{5,3},{6,4},{7,5},{10,8},{11,9},{12,10},{13,11},... | collective-permute-start | bytes 1572872 | tf_op jit(solution)/shard_map/ppermute | solution.py:342
  20.3 33.5 %collective-permute-start.8 = (bf16[128,2048]{1,0:T(8,128)(2,1)}, bf16[128,2048]{1,0:T(8,128)(2,1)S(1)}, u32[]{:S(2)}, u32[]{:S(2)}) collective-permute-start(bf16[128,2048]{1,0:T(8,128)(2,1)} %bitcast.117), channel_id=1, source_target_pairs={{0,1},{1,0},{2,3},{3,2},{4,5},{5,4},{6,7},{7,6},{8,9},{9,8},{10,11... | collective-permute-start | bytes 1572872 | tf_op jit(solution)/shard_map/ppermute | solution.py:347
  25.2 41.2 %all-to-all-start = ((bf16[8,64,512]{2,1,0:T(8,128)(2,1)}), bf16[8,64,512]{2,1,0:T(8,128)(2,1)S(1)}, u32[]{:S(2)}, u32[]{:S(2)}) async-start(bf16[8,64,512]{2,1,0:T(8,128)(2,1)} %squeeze.29), calls=%async_computation | async-start | bytes 1048576 | tf_op jit(solution)/shard_map/all_to_all | solution.py:495
  53.8 60.7 %collective-permute-start.9 = (bf16[128,2048]{1,0:T(8,128)(2,1)}, bf16[128,2048]{1,0:T(8,128)(2,1)}, u32[]{:S(2)}, u32[]{:S(2)}) collective-permute-start(bf16[128,2048]{1,0:T(8,128)(2,1)} %collective-permute-done.6), channel_id=1, source_target_pairs={{2,3},{3,2},{4,5},{5,4},{6,7},{7,6},{10,11},{11,10},{12,13},{13,12... | collective-permute-start | bytes 1572872 | tf_op jit(solution)/shard_map/ppermute | solution.py:347
  55.2 63.1 %collective-permute-start.11 = (bf16[128,2048]{1,0:T(8,128)(2,1)}, bf16[128,2048]{1,0:T(8,128)(2,1)}, u32[]{:S(2)}, u32[]{:S(2)}) collective-permute-start(bf16[128,2048]{1,0:T(8,128)(2,1)} %collective-permute-done.6), channel_id=1, source_target_pairs={{2,4},{3,5},{4,6},{5,7},{10,12},{11,13},{12,14},{13,15},{18,20},{1... | collective-permute-start | bytes 1572872 | tf_op jit(solution)/shard_map/ppermute | solution.py:342
  56.7 59.8 %collective-permute-start.10 = (bf16[128,2048]{1,0:T(8,128)(2,1)}, bf16[128,2048]{1,0:T(8,128)(2,1)}, u32[]{:S(2)}, u32[]{:S(2)}) collective-permute-start(bf16[128,2048]{1,0:T(8,128)(2,1)} %collective-permute-done.7), channel_id=1, source_target_pairs={{0,1},{1,0},{2,3},{3,2},{4,5},{5,4},{8,9},{9,8},{10,11},{11,10},{1... | collective-permute-start | bytes 1572872 | tf_op jit(solution)/shard_map/ppermute | solution.py:347
  59.8 60.5 %collective-permute-start.12 = (bf16[128,2048]{1,0:T(8,128)(2,1)}, bf16[128,2048]{1,0:T(8,128)(2,1)}, u32[]{:S(2)}, u32[]{:S(2)}) collective-permute-start(bf16[128,2048]{1,0:T(8,128)(2,1)} %collective-permute-done.7), channel_id=1, source_target_pairs={{2,0},{3,1},{4,2},{5,3},{10,8},{11,9},{12,10},{13,11},{18,16},{19,... | collective-permute-start | bytes 1572872 | tf_op jit(solution)/shard_map/ppermute | solution.py:342
  61.1 63.1 %collective-permute-start.19 = (bf16[128,2048]{1,0:T(8,128)(2,1)}, bf16[128,2048]{1,0:T(8,128)(2,1)S(1)}, u32[]{:S(2)}, u32[]{:S(2)}) collective-permute-start(bf16[128,2048]{1,0:T(8,128)(2,1)} %param.24), channel_id=1, source_target_pairs={{0,8},{8,0},{16,24},{24,16},{1,9},{9,1},{17,25},{25,17},{2,10},{10... | collective-permute-start | bytes 1572872 | tf_op jit(solution)/shard_map/ppermute | solution.py:302
  67.7 40.4 %all-to-all-start.1 = ((bf16[8,2,128]{2,1,0:T(2,128)(2,1)}), bf16[8,2,128]{2,1,0:T(2,128)(2,1)}, u32[]{:S(2)}, u32[]{:S(2)}) async-start(bf16[8,2,128]{2,1,0:T(2,128)(2,1)} %reshape.127), calls=%async_computation.1 | async-start | bytes 8192 | tf_op jit(solution)/shard_map/all_to_all | solution.py:457
  110.3 34.9 %all-to-all-start.4 = ((bf16[8,64,512]{2,1,0:T(8,128)(2,1)}), bf16[8,64,512]{2,1,0:T(8,128)(2,1)}, u32[]{:S(2)}, u32[]{:S(2)}) async-start(bf16[8,64,512]{2,1,0:T(8,128)(2,1)} %squeeze.28), calls=%async_computation.4 | async-start | bytes 1048576 | tf_op jit(solution)/shard_map/all_to_all | solution.py:522
  126.2 50.5 %collective-permute-start.21 = (bf16[128,2048]{1,0:T(8,128)(2,1)}, bf16[128,2048]{1,0:T(8,128)(2,1)}, u32[]{:S(2)}, u32[]{:S(2)}) collective-permute-start(bf16[128,2048]{1,0:T(8,128)(2,1)} %collective-permute-done.20), channel_id=1, source_target_pairs={{0,8},{8,0},{16,24},{24,16},{1,9},{9,1},{17,25},{25,17},{2,10},{10... | collective-permute-start | bytes 1572872 | tf_op jit(solution)/shard_map/ppermute | solution.py:302
  145.2 36.0 %collective-permute-start.16 = (bf16[512,512]{1,0:T(8,128)(2,1)}, bf16[512,512]{1,0:T(8,128)(2,1)}, u32[]{:S(2)}, u32[]{:S(2)}) collective-permute-start(bf16[512,512]{1,0:T(8,128)(2,1)} %bitcast.20), channel_id=1, source_target_pairs={{0,8},{8,0},{16,24},{24,16},{1,9},{9,1},{17,25},{25,17},{2,10},{10... | collective-permute-start | bytes 1572872 | tf_op jit(solution)/shard_map/ppermute | solution.py:302
  188.5 28.4 %all-to-all-start.3 = ((bf16[8,128,192]{1,2,0:T(8,128)(2,1)}), bf16[8,128,192]{1,2,0:T(8,128)(2,1)}, u32[]{:S(2)}, u32[]{:S(2)}) async-start(bf16[8,128,192]{1,2,0:T(8,128)(2,1)} %broadcast_in_dim.96), calls=%async_computation.3 | async-start | bytes 786432 | tf_op jit(solution)/shard_map/all_to_all | solution.py:457
  205.0 143.9 %reduce-scatter.4.cloned.1.call-start = ((), (), s32[]{:S(2)}) async-start(), calls=%async_computation.12 | async-start | bytes 4718592 | tf_op jit(solution)/shard_map/reduce_scatter | solution.py:570
  256.6 41.3 %collective-permute-start.22 = (bf16[512,512]{1,0:T(8,128)(2,1)}, bf16[512,512]{1,0:T(8,128)(2,1)}, u32[]{:S(2)}, u32[]{:S(2)}) collective-permute-start(bf16[512,512]{1,0:T(8,128)(2,1)} %get-tuple-element.132), channel_id=1, source_target_pairs={{0,8},{8,0},{16,24},{24,16},{1,9},{9,1},{17,25},{25,17},{2,10},{10... | collective-permute-start | bytes 1572872 | tf_op jit(solution)/shard_map/ppermute | solution.py:302
  327.6 30.8 %all-to-all-start.7 = ((bf16[8,64,512]{2,1,0:T(8,128)(2,1)}), bf16[8,64,512]{2,1,0:T(8,128)(2,1)S(1)}, u32[]{:S(2)}, u32[]{:S(2)}) async-start(bf16[8,64,512]{2,1,0:T(8,128)(2,1)} %bitcast.27), calls=%async_computation.8 | async-start | bytes 1048576 | tf_op jit(solution)/shard_map/all_to_all | solution.py:619
  332.3 84.9 %reduce-scatter.6.cloned.1.call-start = ((), (), s32[]{:S(2)}) async-start(), calls=%async_computation.13 | async-start | bytes 798720 | tf_op jit(solution)/shard_map/reduce_scatter | solution.py:640
  342.4 97.6 %reduce-scatter.8.cloned.1.call-start = ((), (), s32[]{:S(2)}) async-start(), calls=%async_computation.14 | async-start | bytes 2621440 | tf_op jit(solution)/shard_map/reduce_scatter | solution.py:621
  364.2 25.6 %collective-permute-start.27 = (bf16[128,2048]{1,0:T(8,128)(2,1)}, bf16[128,2048]{1,0:T(8,128)(2,1)}, u32[]{:S(2)}, u32[]{:S(2)}) collective-permute-start(bf16[128,2048]{1,0:T(8,128)(2,1)} %get-tuple-element.127), channel_id=1, source_target_pairs={{0,1},{1,0},{2,3},{3,2},{4,5},{5,4},{6,7},{7,6},{8,9},{9,8},{10,11... | collective-permute-start | bytes 1572872 | tf_op jit(solution)/shard_map/ppermute | solution.py:347
  365.6 34.6 %collective-permute-start.28 = (bf16[128,2048]{1,0:T(8,128)(2,1)}, bf16[128,2048]{1,0:T(8,128)(2,1)}, u32[]{:S(2)}, u32[]{:S(2)}) collective-permute-start(bf16[128,2048]{1,0:T(8,128)(2,1)} %get-tuple-element.126), channel_id=1, source_target_pairs={{0,1},{1,0},{2,3},{3,2},{4,5},{5,4},{8,9},{9,8},{10,11},{11,10},{1... | collective-permute-start | bytes 1572872 | tf_op jit(solution)/shard_map/ppermute | solution.py:347
  368.2 32.3 %collective-permute-start.29 = (bf16[128,2048]{1,0:T(8,128)(2,1)}, bf16[128,2048]{1,0:T(8,128)(2,1)}, u32[]{:S(2)}, u32[]{:S(2)}) collective-permute-start(bf16[128,2048]{1,0:T(8,128)(2,1)} %get-tuple-element.125), channel_id=1, source_target_pairs={{2,3},{3,2},{4,5},{5,4},{6,7},{7,6},{10,11},{11,10},{12,13},{13,12... | collective-permute-start | bytes 1572872 | tf_op jit(solution)/shard_map/ppermute | solution.py:347
  381.2 26.6 %collective-permute-start.35 = (bf16[512,512]{1,0:T(8,128)(2,1)S(1)}, bf16[512,512]{1,0:T(8,128)(2,1)S(1)}, u32[]{:S(2)}, u32[]{:S(2)}) collective-permute-start(bf16[512,512]{1,0:T(8,128)(2,1)S(1)} %get-tuple-element.131), channel_id=1, source_target_pairs={{0,8},{8,0},{16,24},{24,16},{1,9},{9,1},{17,25},{25,17},{2,10},{10... | collective-permute-start | bytes 1572872 | tf_op jit(solution)/shard_map/ppermute | solution.py:302
  (72 other events, 1220.1 us)
Sparse Core Ops, SparseCore 0:
  10.1 109.2 all-gather.2
  246.2 102.7 reduce-scatter.3
  351.6 20.8 reduce-scatter.5
  376.1 38.3 reduce-scatter.7

commit v2 on v1

--- a/solution.py
+++ b/solution.py
@@ -490,7 +490,9 @@
     states = a_log.shape[1]
     width = own * batch
 
-    halves = in_proj.reshape(in_rows, 2, batch, seq, own).transpose(1, 3, 0, 2, 4)
+    own_gain = norm_gain.astype(f32)[:, None]
+    scaled = (in_proj.astype(f32) * own_gain).astype(bf16)
+    halves = scaled.reshape(in_rows, 2, batch, seq, own).transpose(1, 3, 0, 2, 4)
     halves = halves.reshape(2, seq, in_rows, width)
     columns = lax.all_to_all(halves[0], "seq", 0, 0)
     small = jnp.concatenate(
@@ -502,32 +504,27 @@
             conv_bias[None],
             dt_bias[None],
             skip[None],
-            jnp.pad(norm_gain, (0, own - in_rows))[None],
         ],
         axis=0,
     )
     small = gathered(small, "batch", 1)
     cuts = [rank, 2 * rank + 2 * states, 2 * rank + 3 * states]
-    cuts = cuts + [cuts[2] + taps + i for i in range(4)]
-    delta_weight, select_weight, decay_logs, conv_taps, conv_shift, delta_shift, skip_gain, gain = (
+    cuts = cuts + [cuts[2] + taps + i for i in range(3)]
+    delta_weight, select_weight, decay_logs, conv_taps, conv_shift, delta_shift, skip_gain = (
         jnp.split(small, cuts, axis=0)
     )
     conv_taps, conv_shift = conv_taps.astype(f32), conv_shift.astype(f32)
     delta_shift, skip_gain = delta_shift.astype(f32), skip_gain.astype(f32)
     decay = -jnp.exp(decay_logs.astype(f32))
-    gain = gain.reshape(batch, own)[:, :in_rows]
-    columns, gain = together((columns, gain))
-    gain = shared(gain, "seq")
-    gate_columns, gain = together((halves[1], gain))
+    columns, gate_columns = together((columns, halves[1]))
     gate_columns = lax.all_to_all(gate_columns, "seq", 0, 0)
-    gain = gain.transpose(1, 0, 2).reshape(model).astype(f32)
 
     input_weight = gathered(columns.reshape(seq * in_rows, width), "batch")
 
     def normed(rows):
         rows = rows.astype(f32)
         scale = lax.rsqrt(jnp.mean(rows * rows, axis=-1, keepdims=True) + epsilon)
-        return (rows * scale * gain).astype(bf16)
+        return (rows * scale).astype(bf16)
 
     stream = lax.all_gather(tokens[0], "seq", axis=0, tiled=True)
     gate_weight = gathered(gate_columns.reshape(seq * in_rows, width), "batch")
@@ -639,12 +636,13 @@
     )
     small_grads = lax.psum_scatter(small_grads, "batch", scatter_dimension=1, tiled=True)
     g_dt_proj, g_x_proj, g_log, g_conv, g_conv_bias, g_dt_bias, g_skip = jnp.split(
-        small_grads, cuts[:-1], axis=0
+        small_grads, cuts, axis=0
     )
 
     own_upstream = jnp.where(own_valid, cotangent[0].astype(f32), 0.0)
     own_scale = lax.rsqrt(jnp.mean(own_stream * own_stream, axis=-1, keepdims=True) + epsilon)
-    grad_gain = jnp.sum(grad_input * in_proj.astype(f32), axis=1) / norm_gain.astype(f32)
+    grad_gain = jnp.sum(grad_input * in_proj.astype(f32), axis=1)
+    grad_input = grad_input * own_gain
     (
         d_normalized, g_dt_proj, g_x_proj, g_log, g_conv, g_conv_bias, g_dt_bias, g_skip,
         grad_input, grad_gain, grad_output,
@@ -656,7 +654,7 @@
     )
     for term in last_terms:
         d_normalized = d_normalized + term.astype(f32)
-    d_hat = d_normalized * gain
+    d_hat = d_normalized
     grad_tokens = (
         own_scale * d_hat
         - own_stream

time: 457 us -> 458 us (level)
  waiting for transfers between devices: 115 us -> 125 us
  starting transfers between devices: 106 us -> 98.2 us
  local copies, waits for them, and re-layouts: 68.9 us -> 63.4 us
    ppermute x10, waiting for transfers between devices: 16.2 us -> 52.8 us  [hop(): return lax.ppermute(value, axis, pairs)]
    all_to_all x3 -> x2, waiting for transfers between devices: 40.6 us -> 15 us  [shared(): return lax.all_to_all(wide, axis, 0, 0)]
    all_to_all x3 -> x2, starting transfers between devices: 28.6 us -> 8.52 us  [shared(): return lax.all_to_all(wide, axis, 0, 0)]
    all_to_all x2, starting transfers between devices: 11 us -> 18.1 us  [summed_over_seq(): own = change(jnp.sum(lax.all_to_all(part, 'seq', 0, 0).astype(f32), axis=0))]
    ppermute x10, waiting for transfers between devices: 28.9 us -> 34.3 us  [swap_at(): return lax.ppermute(value, axis, pairs)]
    ppermute x6, waiting for transfers between devices: 17.2 us -> 12.2 us  [outer_shift(): return lax.ppermute(value, axis, pairs)]
  transfers between devices with their start and end apart: 51 -> 50, of which waited for: 18 -> 16; matrix products, arithmetic and copies ran while one was open for 33% -> 32% of each run, Pallas kernels for 7% -> 7%
where the time goes in v2:
time: 458 us; the launch traced here: 453 us
  waiting for transfers between devices  125 us (27%)
  starting transfers between devices  98.2 us (21%)
  local copies, waits for them, and re-layouts  63.4 us (14%)
  matrix products  53.7 us (12%)
  other arithmetic  49.6 us (11%)
  Pallas kernels  47 us (10%)
  between operations  15.7 us (3%)
    dot_general x14, matrix products, matmul(): return lax.dot_general(a, b, dims, preferred_element_type=f32)  53.7 us
    ppermute x10, waiting for transfers between devices, hop(): return lax.ppermute(value, axis, pairs)  52.8 us
    ppermute x10, waiting for transfers between devices, swap_at(): return lax.ppermute(value, axis, pairs)  34.3 us
    pallas_call x1, Pallas kernels, scan_backward(): pl.pallas_call(functools.partial(backward_body, tiles, step), grid=(block...  30.6 us
    ppermute x10, starting transfers between devices, hop(): return lax.ppermute(value, axis, pairs)  25.5 us
    ppermute x10, starting transfers between devices, swap_at(): return lax.ppermute(value, axis, pairs)  21.2 us
    all_to_all x2, starting transfers between devices, summed_over_seq(): own = change(jnp.sum(lax.all_to_all(part, 'seq', 0, 0).astype(f32), axis=0))  18.1 us
    pallas_call x1, Pallas kernels, scan_forward(): pl.pallas_call(functools.partial(forward_body, tiles, step), grid=(length...  16.4 us
  transfers between devices with their start and end apart: 50, of which 16 were waited for; matrix products, arithmetic and copies ran while one was open for 32% of the time, Pallas kernels for 7%

profile of v2, /device:TPU:0, one launch (start us, length us, event | category | flops | bytes accessed | tf_op | source)
XLA Modules:
  0.0 452.9 jit_solution(4157138590117739292)
XLA Ops:
  25.5 5.9 %all-to-all-start = ((bf16[8,64,512]{2,1,0:T(8,128)(2,1)}), bf16[8,64,512]{2,1,0:T(8,128)(2,1)S(1)}, u32[]{:S(2)}, u32[]{:S(2)}) async-start(bf16[8,64,512]{2,1,0:T(8,128)(2,1)} %squeeze.28), calls=%async_computation | async-start | bytes 1048576 | tf_op jit(solution)/shard_map/all_to_all | solution.py:497
  39.3 15.2 %collective-permute-done.7 = bf16[128,2048]{1,0:T(8,128)(2,1)} collective-permute-done((bf16[128,2048]{1,0:T(8,128)(2,1)}, bf16[128,2048]{1,0:T(8,128)(2,1)}, u32[]{:S(2)}, u32[]{:S(2)}) %collective-permute-start.7) | collective-permute-done | bytes 524320 | tf_op jit(solution)/shard_map/ppermute | solution.py:342
  67.2 6.1 %all-to-all-start.3 = ((bf16[8,64,512]{2,1,0:T(8,128)(2,1)}), bf16[8,64,512]{2,1,0:T(8,128)(2,1)}, u32[]{:S(2)}, u32[]{:S(2)}) async-start(bf16[8,64,512]{2,1,0:T(8,128)(2,1)} %squeeze.29), calls=%async_computation.3 | async-start | bytes 1048576 | tf_op jit(solution)/shard_map/all_to_all | solution.py:520
  81.7 11.5 %collective-permute-done.12 = bf16[128,2048]{1,0:T(8,128)(2,1)} collective-permute-done((bf16[128,2048]{1,0:T(8,128)(2,1)}, bf16[128,2048]{1,0:T(8,128)(2,1)}, u32[]{:S(2)}, u32[]{:S(2)}) %collective-permute-start.12) | collective-permute-done | bytes 524320 | tf_op jit(solution)/shard_map/ppermute | solution.py:342
  104.0 26.1 %collective-permute-done.14 = bf16[128,2048]{1,0:T(8,128)(2,1)} collective-permute-done((bf16[128,2048]{1,0:T(8,128)(2,1)S(1)}, bf16[128,2048]{1,0:T(8,128)(2,1)}, u32[]{:S(2)}, u32[]{:S(2)}) %collective-permute-start.14) | collective-permute-done | bytes 524320 | tf_op jit(solution)/shard_map/ppermute | solution.py:342
  137.8 6.4 %collective-permute-done.15 = bf16[128,2048]{1,0:T(8,128)(2,1)S(1)} collective-permute-done((bf16[128,2048]{1,0:T(8,128)(2,1)}, bf16[128,2048]{1,0:T(8,128)(2,1)S(1)}, u32[]{:S(2)}, u32[]{:S(2)}) %collective-permute-start.15) | collective-permute-done | bytes 524320 | tf_op jit(solution)/shard_map/ppermute | solution.py:347
  146.2 5.3 %collective-permute-done.17 = bf16[512,512]{1,0:T(8,128)(2,1)} collective-permute-done((bf16[512,512]{1,0:T(8,128)(2,1)}, bf16[512,512]{1,0:T(8,128)(2,1)}, u32[]{:S(2)}, u32[]{:S(2)}) %collective-permute-start.17) | collective-permute-done | bytes 524320 | tf_op jit(solution)/shard_map/ppermute | solution.py:309
  178.0 4.9 %all-to-all-start.2 = ((bf16[8,128,192]{1,2,0:T(8,128)(2,1)}), bf16[8,128,192]{1,2,0:T(8,128)(2,1)}, u32[]{:S(2)}, u32[]{:S(2)}) async-start(bf16[8,128,192]{1,2,0:T(8,128)(2,1)} %broadcast_in_dim.84), calls=%async_computation.2 | async-start | bytes 786432 | tf_op jit(solution)/shard_map/all_to_all | solution.py:457
  183.3 6.2 %convolution_convert_fusion.4 = bf16[1024,512]{1,0:T(8,128)(2,1)} fusion(bf16[2048,512]{1,0:T(8,128)(2,1)} %constant_dynamic-update-slice_fusion.4, bf16[1,1024,2048]{2,1,0:T(8,128)(2,1)} %all-gather.3.cloned.1.call-done, f32[1024]{0:T(1024)} %copy-done.35), kind=kOutput, calls=%fused_computation.69 | convolution fusion | flops 2154299392 | bytes 7344128 | tf_op jit(solution)/shard_map/dot_general | solution.py:461
  189.5 5.9 %fusion.35 = f32[1024,512]{1,0:T(8,128)} fusion(bf16[512,2048]{1,0:T(8,128)(2,1)S(1)} %constant_dynamic-update-slice_fusion, bf16[1024,2048]{1,0:T(8,128)(2,1)} %select_dynamic-update-slice_fusion, pred[1024]{0:T(1024)(128)(4,1)S(1)} %copy-done.40), kind=kOutput, calls=%fused_computation.68 | convolution fusion | flops 2149580800 | bytes 8389632 | tf_op jit(solution)/shard_map/dot_general | solution.py:461
  200.6 16.4 %scan_forward.1 = (f32[1024,512]{1,0:T(8,128)S(1)}, bf16[16384,512]{1,0:T(8,128)(2,1)}) custom-call(f32[1024,512]{1,0:T(8,128)S(1)} %get-tuple-element.149.delta, bf16[1024,512]{1,0:T(8,128)(2,1)S(1)} %multiply_convert_fusion.1.active, bf16[1024,192]{1,0:T(8,128)(2,1)S(1)} %bitcast.100, f32[16,512]{1,0:T(8,128)S(1)} %get-tuple-element.138.rate), custom_call_target="tpu_custom_call" | custom-call | flops 67108864 | bytes 22020096 | tf_op jit(solution)/shard_map/scan_forward/pallas_call | solution.py:90
  220.3 4.4 convolution_convert_fusion
  224.7 6.7 %fusion.15 = (f32[512]{0:T(512)}, f32[1024,512]{1,0:T(8,128)}, bf16[1024,512]{1,0:T(8,128)(2,1)S(1)}) fusion(f32[1024,512]{1,0:T(8,128)} %fusion.35, bf16[1024,512]{1,0:T(8,128)(2,1)} %convolution_convert_fusion.4, f32[1024,512]{1,0:T(8,128)S(1)} %get-tuple-element.67, f32[512]{0:T(512)S(1)} %bitcast.144, bf16[1024,512]{1,0:T(8,128)(2,1)} %copy-done.4, ...), kind=kLoop, calls=%fused_computation.40 | loop fusion | flops 18349568 | bytes 9451520 | tf_op jit(solution)/shard_map/reduce_sum | solution.py:573
  235.7 30.6 %scan_backward.1 = (f32[1024,512]{1,0:T(8,128)S(1)}, f32[1024,512]{1,0:T(8,128)}, f32[1024,32]{1,0:T(8,128)S(1)}, f32[16,512]{1,0:T(8,128)S(1)}) custom-call(f32[1024,512]{1,0:T(8,128)} %copy-done.3, bf16[1024,512]{1,0:T(8,128)(2,1)S(1)} %multiply_convert_fusion.1.active, f32[1024,512]{1,0:T(8,128)} %get-tuple-element.110.d_mixed, ...), custom_call_target="tpu_custom_call" | custom-call | flops 167772160 | bytes 27262976 | tf_op jit(solution)/shard_map/scan_backward/pallas_call | solution.py:251
  270.7 14.7 %all-to-all-start.4 = ((bf16[8,128,160]{1,2,0:T(8,128)(2,1)}), bf16[8,128,160]{1,2,0:T(8,128)(2,1)S(1)}, u32[]{:S(2)}, u32[]{:S(2)}) async-start(bf16[8,128,160]{1,2,0:T(8,128)(2,1)} %pad_maximum_fusion.1), calls=%async_computation.4 | async-start | bytes 655360 | tf_op jit(solution)/shard_map/all_to_all | solution.py:446
  287.8 8.0 %all-to-all-done.4 = bf16[8,128,160]{1,2,0:T(8,128)(2,1)S(1)} async-done(((bf16[8,128,160]{1,2,0:T(8,128)(2,1)}), bf16[8,128,160]{1,2,0:T(8,128)(2,1)S(1)}, u32[]{:S(2)}, u32[]{:S(2)}) %all-to-all-start.4) | async-done | bytes 327712 | tf_op jit(solution)/shard_map/all_to_all | solution.py:446
  304.5 15.0 %all-to-all-done.5 = bf16[8,128,160]{1,2,0:T(8,128)(2,1)S(1)} async-done(((bf16[8,128,160]{1,2,0:T(8,128)(2,1)}), bf16[8,128,160]{1,2,0:T(8,128)(2,1)S(1)}, u32[]{:S(2)}, u32[]{:S(2)}) %all-to-all-start.5) | async-done | bytes 327712 | tf_op jit(solution)/shard_map/all_to_all | solution.py:457
  333.2 5.1 %convolution_convert_fusion.2 = bf16[2048,512]{1,0:T(8,128)(2,1)S(1)} fusion(bf16[1024,512]{1,0:T(8,128)(2,1)} %get-tuple-element.77, bf16[1,1024,2048]{2,1,0:T(8,128)(2,1)} %all-gather.3.cloned.1.call-done, f32[1024]{0:T(1024)S(1)} %copy-done.37), kind=kOutput, calls=%fused_computation.23 | convolution fusion | flops 2154823680 | bytes 7344128 | tf_op jit(solution)/shard_map/dot_general | solution.py:461
  338.3 9.5 %fusion.6 = bf16[1024,2048]{1,0:T(8,128)(2,1)} fusion(bf16[2048,512]{1,0:T(8,128)(2,1)} %constant_dynamic-update-slice_fusion.4, bf16[2048,512]{1,0:T(8,128)(2,1)} %constant_dynamic-update-slice_fusion.16, bf16[1024,512]{1,0:T(8,128)(2,1)} %copy-done.25, bf16[1024,512]{1,0:T(8,128)(2,1)} %get-tuple-element.77), kind=kOutput, calls=%fused_computation.16 | convolution fusion | flops 4309647360 | bytes 10485760 | tf_op jit(solution)/shard_map/dot_general | solution.py:461
  347.9 6.6 %convolution_convert_fusion.1 = bf16[512,2048]{1,0:T(8,128)(2,1)} fusion(bf16[1024,512]{1,0:T(8,128)(2,1)} %copy-done.24, bf16[1024,2048]{1,0:T(8,128)(2,1)} %select_dynamic-update-slice_fusion, pred[1024]{0:T(1024)(128)(4,1)S(1)} %copy-done.41), kind=kOutput, calls=%fused_computation.22 | convolution fusion | flops 2150629376 | bytes 7341056 | tf_op jit(solution)/shard_map/dot_general | solution.py:461
  366.4 8.2 %collective-permute-done.25 = bf16[128,2048]{1,0:T(8,128)(2,1)} collective-permute-done((bf16[128,2048]{1,0:T(8,128)(2,1)}, bf16[128,2048]{1,0:T(8,128)(2,1)}, u32[]{:S(2)}, u32[]{:S(2)}) %collective-permute-start.25) | collective-permute-done | bytes 524320 | tf_op jit(solution)/shard_map/ppermute | solution.py:347
  379.3 6.3 %collective-permute-done.27 = bf16[128,2048]{1,0:T(8,128)(2,1)S(1)} collective-permute-done((bf16[128,2048]{1,0:T(8,128)(2,1)}, bf16[128,2048]{1,0:T(8,128)(2,1)S(1)}, u32[]{:S(2)}, u32[]{:S(2)}) %collective-permute-start.27) | collective-permute-done | bytes 524320 | tf_op jit(solution)/shard_map/ppermute | solution.py:347
  385.7 11.3 %collective-permute-done.28 = bf16[128,2048]{1,0:T(8,128)(2,1)} collective-permute-done((bf16[128,2048]{1,0:T(8,128)(2,1)}, bf16[128,2048]{1,0:T(8,128)(2,1)}, u32[]{:S(2)}, u32[]{:S(2)}) %collective-permute-start.28) | collective-permute-done | bytes 524320 | tf_op jit(solution)/shard_map/ppermute | solution.py:347
  423.7 8.1 %collective-permute-start.36 = (bf16[128,2048]{1,0:T(8,128)(2,1)}, bf16[128,2048]{1,0:T(8,128)(2,1)}, u32[]{:S(2)}, u32[]{:S(2)}) collective-permute-start(bf16[128,2048]{1,0:T(8,128)(2,1)} %get-tuple-element.117), channel_id=1, source_target_pairs={{0,2},{1,3},{2,4},{3,5},{4,6},{5,7},{8,10},{9,11},{10,12},{11,13},... | collective-permute-start | bytes 1572872 | tf_op jit(solution)/shard_map/ppermute | solution.py:342
  (273 shorter events, 192.7 us)
Async XLA Ops:
  7.2 144.3 %all-gather.3.cloned.1.call-start = ((), (), s32[]{:S(2)}) async-start(), calls=%async_computation.14 | async-start | bytes 4718592 | tf_op jit(solution)/shard_map/all_gather | solution.py:529
  10.9 26.4 %collective-permute-start = (bf16[311,128]{1,0:T(8,128)(2,1)S(1)}, bf16[311,128]{1,0:T(8,128)(2,1)S(1)}, u32[]{:S(2)}, u32[]{:S(2)}) collective-permute-start(bf16[311,128]{1,0:T(8,128)(2,1)S(1)} %concatenate.30), channel_id=1, source_target_pairs={{0,8},{8,0},{16,24},{24,16},{1,9},{9,1},{17,25},{25,17},{2,10},{10... | collective-permute-start | bytes 238856 | tf_op jit(solution)/shard_map/ppermute | solution.py:302
  11.4 25.9 %collective-permute-start.1 = (bf16[311,128]{1,0:T(8,128)(2,1)S(1)}, bf16[311,128]{1,0:T(8,128)(2,1)S(1)}, u32[]{:S(2)}, u32[]{:S(2)}) collective-permute-start(bf16[311,128]{1,0:T(8,128)(2,1)S(1)} %concatenate.30), channel_id=1, source_target_pairs={{0,16},{8,24},{16,0},{24,8},{1,17},{9,25},{17,1},{25,9},{2,18},{10... | collective-permute-start | bytes 238856 | tf_op jit(solution)/shard_map/ppermute | solution.py:309
  18.3 36.2 %collective-permute-start.7 = (bf16[128,2048]{1,0:T(8,128)(2,1)}, bf16[128,2048]{1,0:T(8,128)(2,1)}, u32[]{:S(2)}, u32[]{:S(2)}) collective-permute-start(bf16[128,2048]{1,0:T(8,128)(2,1)} %bitcast.108), channel_id=1, source_target_pairs={{2,0},{3,1},{4,2},{5,3},{6,4},{7,5},{10,8},{11,9},{12,10},{13,11},... | collective-permute-start | bytes 1572872 | tf_op jit(solution)/shard_map/ppermute | solution.py:342
  19.6 34.9 %collective-permute-start.8 = (bf16[128,2048]{1,0:T(8,128)(2,1)}, bf16[128,2048]{1,0:T(8,128)(2,1)S(1)}, u32[]{:S(2)}, u32[]{:S(2)}) collective-permute-start(bf16[128,2048]{1,0:T(8,128)(2,1)} %bitcast.109), channel_id=1, source_target_pairs={{0,1},{1,0},{2,3},{3,2},{4,5},{5,4},{6,7},{7,6},{8,9},{9,8},{10,11... | collective-permute-start | bytes 1572872 | tf_op jit(solution)/shard_map/ppermute | solution.py:347
  25.5 41.7 %all-to-all-start = ((bf16[8,64,512]{2,1,0:T(8,128)(2,1)}), bf16[8,64,512]{2,1,0:T(8,128)(2,1)S(1)}, u32[]{:S(2)}, u32[]{:S(2)}) async-start(bf16[8,64,512]{2,1,0:T(8,128)(2,1)} %squeeze.28), calls=%async_computation | async-start | bytes 1048576 | tf_op jit(solution)/shard_map/all_to_all | solution.py:497
  55.9 25.8 %collective-permute-start.11 = (bf16[128,2048]{1,0:T(8,128)(2,1)}, bf16[128,2048]{1,0:T(8,128)(2,1)}, u32[]{:S(2)}, u32[]{:S(2)}) collective-permute-start(bf16[128,2048]{1,0:T(8,128)(2,1)} %collective-permute-done.6), channel_id=1, source_target_pairs={{2,4},{3,5},{4,6},{5,7},{10,12},{11,13},{12,14},{13,15},{18,20},{1... | collective-permute-start | bytes 1572872 | tf_op jit(solution)/shard_map/ppermute | solution.py:342
  60.6 32.6 %collective-permute-start.12 = (bf16[128,2048]{1,0:T(8,128)(2,1)}, bf16[128,2048]{1,0:T(8,128)(2,1)}, u32[]{:S(2)}, u32[]{:S(2)}) collective-permute-start(bf16[128,2048]{1,0:T(8,128)(2,1)} %collective-permute-done.7), channel_id=1, source_target_pairs={{2,0},{3,1},{4,2},{5,3},{10,8},{11,9},{12,10},{13,11},{18,16},{19,... | collective-permute-start | bytes 1572872 | tf_op jit(solution)/shard_map/ppermute | solution.py:342
  61.9 34.0 %collective-permute-start.19 = (bf16[128,2048]{1,0:T(8,128)(2,1)}, bf16[128,2048]{1,0:T(8,128)(2,1)S(1)}, u32[]{:S(2)}, u32[]{:S(2)}) collective-permute-start(bf16[128,2048]{1,0:T(8,128)(2,1)} %param.24), channel_id=1, source_target_pairs={{0,8},{8,0},{16,24},{24,16},{1,9},{9,1},{17,25},{25,17},{2,10},{10... | collective-permute-start | bytes 1572872 | tf_op jit(solution)/shard_map/ppermute | solution.py:302
  67.2 69.6 %all-to-all-start.3 = ((bf16[8,64,512]{2,1,0:T(8,128)(2,1)}), bf16[8,64,512]{2,1,0:T(8,128)(2,1)}, u32[]{:S(2)}, u32[]{:S(2)}) async-start(bf16[8,64,512]{2,1,0:T(8,128)(2,1)} %squeeze.29), calls=%async_computation.3 | async-start | bytes 1048576 | tf_op jit(solution)/shard_map/all_to_all | solution.py:520
  95.2 38.6 %collective-permute-start.13 = (bf16[128,2048]{1,0:T(8,128)(2,1)S(1)}, bf16[128,2048]{1,0:T(8,128)(2,1)S(1)}, u32[]{:S(2)}, u32[]{:S(2)}) collective-permute-start(bf16[128,2048]{1,0:T(8,128)(2,1)S(1)} %get-tuple-element.116), channel_id=1, source_target_pairs={{0,1},{1,0},{2,3},{3,2},{4,5},{5,4},{6,7},{7,6},{8,9},{9,8},{10,11... | collective-permute-start | bytes 1572872 | tf_op jit(solution)/shard_map/ppermute | solution.py:347
  96.0 34.2 %collective-permute-start.14 = (bf16[128,2048]{1,0:T(8,128)(2,1)S(1)}, bf16[128,2048]{1,0:T(8,128)(2,1)}, u32[]{:S(2)}, u32[]{:S(2)}) collective-permute-start(bf16[128,2048]{1,0:T(8,128)(2,1)S(1)} %get-tuple-element.116), channel_id=1, source_target_pairs={{4,6},{5,7},{2,0},{3,1},{12,14},{13,15},{10,8},{11,9},{20,22},{21,... | collective-permute-start | bytes 1572872 | tf_op jit(solution)/shard_map/ppermute | solution.py:342
  97.3 68.7 %collective-permute-start.21 = (bf16[128,2048]{1,0:T(8,128)(2,1)}, bf16[128,2048]{1,0:T(8,128)(2,1)}, u32[]{:S(2)}, u32[]{:S(2)}) collective-permute-start(bf16[128,2048]{1,0:T(8,128)(2,1)} %collective-permute-done.20), channel_id=1, source_target_pairs={{0,8},{8,0},{16,24},{24,16},{1,9},{9,1},{17,25},{25,17},{2,10},{10... | collective-permute-start | bytes 1572872 | tf_op jit(solution)/shard_map/ppermute | solution.py:302
  101.3 35.7 %collective-permute-start.5 = (bf16[512,512]{1,0:T(8,128)(2,1)}, bf16[512,512]{1,0:T(8,128)(2,1)S(1)}, u32[]{:S(2)}, u32[]{:S(2)}) collective-permute-start(bf16[512,512]{1,0:T(8,128)(2,1)} %collective-permute-done.4), channel_id=1, source_target_pairs={{0,8},{8,0},{16,24},{24,16},{1,9},{9,1},{17,25},{25,17},{2,10},{10... | collective-permute-start | bytes 1572872 | tf_op jit(solution)/shard_map/ppermute | solution.py:302
  136.8 33.8 %collective-permute-start.16 = (bf16[512,512]{1,0:T(8,128)(2,1)}, bf16[512,512]{1,0:T(8,128)(2,1)}, u32[]{:S(2)}, u32[]{:S(2)}) collective-permute-start(bf16[512,512]{1,0:T(8,128)(2,1)} %bitcast.18), channel_id=1, source_target_pairs={{0,8},{8,0},{16,24},{24,16},{1,9},{9,1},{17,25},{25,17},{2,10},{10... | collective-permute-start | bytes 1572872 | tf_op jit(solution)/shard_map/ppermute | solution.py:302
  183.0 155.3 %reduce-scatter.4.cloned.1.call-start = ((), (), s32[]{:S(2)}) async-start(), calls=%async_computation.11 | async-start | bytes 4718592 | tf_op jit(solution)/shard_map/reduce_scatter | solution.py:567
  235.1 50.2 %collective-permute-start.22 = (bf16[512,512]{1,0:T(8,128)(2,1)}, bf16[512,512]{1,0:T(8,128)(2,1)}, u32[]{:S(2)}, u32[]{:S(2)}) collective-permute-start(bf16[512,512]{1,0:T(8,128)(2,1)} %get-tuple-element.128), channel_id=1, source_target_pairs={{0,8},{8,0},{16,24},{24,16},{1,9},{9,1},{17,25},{25,17},{2,10},{10... | collective-permute-start | bytes 1572872 | tf_op jit(solution)/shard_map/ppermute | solution.py:302
  319.6 28.3 %all-to-all-start.6 = ((bf16[8,64,512]{2,1,0:T(8,128)(2,1)}), bf16[8,64,512]{2,1,0:T(8,128)(2,1)S(1)}, u32[]{:S(2)}, u32[]{:S(2)}) async-start(bf16[8,64,512]{2,1,0:T(8,128)(2,1)} %bitcast.25), calls=%async_computation.7 | async-start | bytes 1048576 | tf_op jit(solution)/shard_map/all_to_all | solution.py:616
  323.1 89.9 %reduce-scatter.6.cloned.1.call-start = ((), (), s32[]{:S(2)}) async-start(), calls=%async_computation.12 | async-start | bytes 798720 | tf_op jit(solution)/shard_map/reduce_scatter | solution.py:637
  333.2 106.3 %reduce-scatter.8.cloned.1.call-start = ((), (), s32[]{:S(2)}) async-start(), calls=%async_computation.13 | async-start | bytes 2621440 | tf_op jit(solution)/shard_map/reduce_scatter | solution.py:618
  361.7 35.3 %collective-permute-start.28 = (bf16[128,2048]{1,0:T(8,128)(2,1)}, bf16[128,2048]{1,0:T(8,128)(2,1)}, u32[]{:S(2)}, u32[]{:S(2)}) collective-permute-start(bf16[128,2048]{1,0:T(8,128)(2,1)} %get-tuple-element.122), channel_id=1, source_target_pairs={{0,1},{1,0},{2,3},{3,2},{4,5},{5,4},{8,9},{9,8},{10,11},{11,10},{1... | collective-permute-start | bytes 1572872 | tf_op jit(solution)/shard_map/ppermute | solution.py:347
  365.5 32.2 %collective-permute-start.29 = (bf16[128,2048]{1,0:T(8,128)(2,1)S(1)}, bf16[128,2048]{1,0:T(8,128)(2,1)S(1)}, u32[]{:S(2)}, u32[]{:S(2)}) collective-permute-start(bf16[128,2048]{1,0:T(8,128)(2,1)S(1)} %get-tuple-element.121), channel_id=1, source_target_pairs={{2,3},{3,2},{4,5},{5,4},{6,7},{7,6},{10,11},{11,10},{12,13},{13,12... | collective-permute-start | bytes 1572872 | tf_op jit(solution)/shard_map/ppermute | solution.py:347
  377.2 41.3 %collective-permute-start.32 = (bf16[128,2048]{1,0:T(8,128)(2,1)S(1)}, bf16[128,2048]{1,0:T(8,128)(2,1)}, u32[]{:S(2)}, u32[]{:S(2)}) collective-permute-start(bf16[128,2048]{1,0:T(8,128)(2,1)S(1)} %get-tuple-element.120), channel_id=1, source_target_pairs={{0,1},{1,0},{2,3},{3,2},{4,5},{5,4},{6,7},{7,6},{8,9},{9,8},{10,11... | collective-permute-start | bytes 1572872 | tf_op jit(solution)/shard_map/ppermute | solution.py:347
  408.7 26.3 %all-to-all-start.7 = ((bf16[8,64,512]{2,1,0:T(8,128)(2,1)}), bf16[8,64,512]{2,1,0:T(8,128)(2,1)}, u32[]{:S(2)}, u32[]{:S(2)}) async-start(bf16[8,64,512]{2,1,0:T(8,128)(2,1)} %bitcast.33), calls=%async_computation.9 | async-start | bytes 1048576 | tf_op jit(solution)/shard_map/all_to_all | solution.py:630
  (68 other events, 1035.7 us)
Sparse Core Ops, SparseCore 0:
  10.1 113.4 all-gather.2
  224.8 96.3 reduce-scatter.3
  333.3 23.1 reduce-scatter.5
  359.0 31.9 reduce-scatter.7

commit v3 on v1

--- a/solution.py
+++ b/solution.py
@@ -350,9 +350,9 @@
 UP, DOWN = [(0, 1), (1, 2), (2, 3)], [(1, 0), (2, 1), (3, 2)]
 
 
-def line_gathered(own, axis, held):
+def line_gathered(own, axis):
     if lax.axis_size(axis) != 8:
-        return lax.all_gather(own, axis, axis=0, tiled=True), held
+        return lax.all_gather(own, axis, axis=0, tiled=True)
     place = lax.axis_index(axis)
     z, x = place // 2, place % 2
     rows = own.shape[0]
@@ -368,9 +368,7 @@
         return put(whole, jnp.where(edge, piece, held), far, side)
 
     whole = jnp.zeros((8 * rows,) + own.shape[1:], own.dtype)
-    up, down, other, held = together(
-        (hop(own, axis, UP), hop(own, axis, DOWN), swap_at(own, axis, range(4)), held)
-    )
+    up, down, other = hop(own, axis, UP), hop(own, axis, DOWN), swap_at(own, axis, range(4))
     up_two, down_two = hop(up, axis, UP[1:]), hop(down, axis, DOWN[:2])
     other_up, other_down = swap_at(up, axis, (1, 2, 3)), swap_at(down, axis, (0, 1, 2))
     whole = put(put(whole, own, z, x), other, z, 1 - x)
@@ -382,7 +380,7 @@
     whole = put(whole, two, across, x)
     other_three = swap_at(three, axis, (0, 3))
     whole = put(whole, other_two, across, 1 - x)
-    return put_far(put_far(whole, three, x), other_three, 1 - x), held
+    return put_far(put_far(whole, three, x), other_three, 1 - x)
 
 
 def line_summed(part_of, axis):
@@ -490,9 +488,8 @@
     states = a_log.shape[1]
     width = own * batch
 
-    halves = in_proj.reshape(in_rows, 2, batch, seq, own).transpose(1, 3, 0, 2, 4)
-    halves = halves.reshape(2, seq, in_rows, width)
-    columns = lax.all_to_all(halves[0], "seq", 0, 0)
+    columns = in_proj.reshape(in_rows, 2, batch, seq, own).transpose(3, 0, 1, 2, 4)
+    columns = lax.all_to_all(columns.reshape(seq, in_rows, 2 * width), "seq", 0, 0)
     small = jnp.concatenate(
         [
             dt_proj,
@@ -516,13 +513,9 @@
     delta_shift, skip_gain = delta_shift.astype(f32), skip_gain.astype(f32)
     decay = -jnp.exp(decay_logs.astype(f32))
     gain = gain.reshape(batch, own)[:, :in_rows]
-    columns, gain = together((columns, gain))
-    gain = shared(gain, "seq")
-    gate_columns, gain = together((halves[1], gain))
-    gate_columns = lax.all_to_all(gate_columns, "seq", 0, 0)
-    gain = gain.transpose(1, 0, 2).reshape(model).astype(f32)
-
-    input_weight = gathered(columns.reshape(seq * in_rows, width), "batch")
+    columns, gain, out_proj = together((columns, gain, out_proj))
+    gain = shared(gain, "seq").transpose(1, 0, 2).reshape(model).astype(f32)
+    weight = gathered(columns.reshape(seq * in_rows, 2 * width), "batch")
 
     def normed(rows):
         rows = rows.astype(f32)
@@ -530,13 +523,12 @@
         return (rows * scale * gain).astype(bf16)
 
     stream = lax.all_gather(tokens[0], "seq", axis=0, tiled=True)
-    gate_weight = gathered(gate_columns.reshape(seq * in_rows, width), "batch")
     normalized = normed(stream)
-    upstream, out_proj = line_gathered(cotangent[0], "seq", out_proj)
+    upstream = line_gathered(cotangent[0], "seq")
     output_weight = gathered(out_proj, "batch")
 
     valid = (jnp.arange(length, dtype=jnp.int32) < lengths[0])[:, None]
-    inner = matmul(normalized, input_weight).astype(bf16)
+    inner = matmul(normalized, weight[:, :width]).astype(bf16)
     padded = jnp.pad(inner, ((taps - 1, 0), (0, 0)))
     conv_out = conv_shift + jnp.zeros((length, width), f32)
     for tap in range(taps):
@@ -550,7 +542,7 @@
         lambda s: jnp.concatenate([s[:, :rank].astype(bf16)] + two_terms(s[:, rank:]), axis=1),
     )
     upstream = jnp.where(valid, upstream, 0).astype(bf16)
-    gate_low = matmul(normalized, gate_weight).astype(bf16)
+    gate_low = matmul(normalized, weight[:, width:]).astype(bf16)
     d_gated = matmul(upstream, output_weight, NT)
     select, gate_low, d_gated = together((select, gate_low, d_gated))
     gate = gate_low.astype(f32)
@@ -611,7 +603,7 @@
     d_inner, grad_inner, branch = together((d_inner, grad_inner, branch))
     d_normalized = matmul(
         jnp.concatenate([d_inner, d_gate_low], axis=1),
-        jnp.concatenate([input_weight, gate_weight], axis=1),
+        weight,
         NT,
     ).astype(bf16)
     grad_inner = scattered_sum(rows_of(grad_inner, model // batch), "batch")

time: 457 us -> 473 us (1.035)
  waiting for transfers between devices: 115 us -> 146 us
  local copies, waits for them, and re-layouts: 68.9 us -> 61.5 us
  starting transfers between devices: 106 us -> 99.9 us
    ppermute x10, waiting for transfers between devices: 16.2 us -> 64.4 us  [hop(): return lax.ppermute(value, axis, pairs)]
    all_to_all x3, waiting for transfers between devices: 40.6 us -> 19 us  [shared(): return lax.all_to_all(wide, axis, 0, 0)]
    all_to_all x3, starting transfers between devices: 28.6 us -> 11.2 us  [shared(): return lax.all_to_all(wide, axis, 0, 0)]
    all_to_all x2, starting transfers between devices: 11 us -> 18.8 us  [summed_over_seq(): own = change(jnp.sum(lax.all_to_all(part, 'seq', 0, 0).astype(f32), axis=0))]
    dynamic_update_slice x16 -> x12, local copies, waits for them, and re-layouts: 16.3 us -> 10.2 us  [gathered(): whole = lax.dynamic_update_slice_in_dim(whole, piece, place * size, dim)]
    all_to_all x2 -> x1, starting transfers between devices: 10 us -> 5.92 us  [on_device(): lax.all_to_all(columns.reshape(seq, in_rows, 2 * width), 'seq', 0, 0)]
    ppermute x6 -> x5, waiting for transfers between devices: 17.2 us -> 16.3 us  [outer_shift(): return lax.ppermute(value, axis, pairs)]
  transfers between devices with their start and end apart: 51 -> 47, of which waited for: 18 -> 17; matrix products, arithmetic and copies ran while one was open for 33% -> 27% of each run, Pallas kernels for 7% -> 7%
where the time goes in v3:
time: 473 us; the launch traced here: 469 us
  waiting for transfers between devices  146 us (31%)
  starting transfers between devices  99.9 us (21%)
  local copies, waits for them, and re-layouts  61.5 us (13%)
  matrix products  52.5 us (11%)
  Pallas kernels  47.4 us (10%)
  other arithmetic  46.4 us (10%)
  between operations  15.7 us (3%)
    ppermute x10, waiting for transfers between devices, hop(): return lax.ppermute(value, axis, pairs)  64.4 us
    dot_general x14, matrix products, matmul(): return lax.dot_general(a, b, dims, preferred_element_type=f32)  52.5 us
    pallas_call x1, Pallas kernels, scan_backward(): pl.pallas_call(functools.partial(backward_body, tiles, step), grid=(block...  31 us
    ppermute x10, waiting for transfers between devices, swap_at(): return lax.ppermute(value, axis, pairs)  31 us
    ppermute x10, starting transfers between devices, hop(): return lax.ppermute(value, axis, pairs)  25.2 us
    ppermute x10, starting transfers between devices, swap_at(): return lax.ppermute(value, axis, pairs)  22.8 us
    all_to_all x3, waiting for transfers between devices, shared(): return lax.all_to_all(wide, axis, 0, 0)  19 us
    all_to_all x2, starting transfers between devices, summed_over_seq(): own = change(jnp.sum(lax.all_to_all(part, 'seq', 0, 0).astype(f32), axis=0))  18.8 us
  transfers between devices with their start and end apart: 47, of which 17 were waited for; matrix products, arithmetic and copies ran while one was open for 27% of the time, Pallas kernels for 7%

profile of v3, /device:TPU:0, one launch (start us, length us, event | category | flops | bytes accessed | tf_op | source)
XLA Modules:
  0.0 469.0 jit_solution(1330375810837590690)
XLA Ops:
  24.4 5.9 %all-to-all-start = ((bf16[8,64,1024]{2,1,0:T(8,128)(2,1)}), bf16[8,64,1024]{2,1,0:T(8,128)(2,1)S(1)}, u32[]{:S(2)}, u32[]{:S(2)}) async-start(bf16[8,64,1024]{2,1,0:T(8,128)(2,1)} %reshape.106), calls=%async_computation | async-start | bytes 2097152 | tf_op jit(solution)/shard_map/all_to_all | solution.py:492
  36.4 6.3 %collective-permute-done.7 = bf16[128,2048]{1,0:T(8,128)(2,1)S(1)} collective-permute-done((bf16[128,2048]{1,0:T(8,128)(2,1)}, bf16[128,2048]{1,0:T(8,128)(2,1)S(1)}, u32[]{:S(2)}, u32[]{:S(2)}) %collective-permute-start.7) | collective-permute-done | bytes 524320 | tf_op jit(solution)/shard_map/ppermute | solution.py:342
  44.0 8.3 %collective-permute-done.8 = bf16[128,2048]{1,0:T(8,128)(2,1)S(1)} collective-permute-done((bf16[128,2048]{1,0:T(8,128)(2,1)}, bf16[128,2048]{1,0:T(8,128)(2,1)S(1)}, u32[]{:S(2)}, u32[]{:S(2)}) %collective-permute-start.8) | collective-permute-done | bytes 524320 | tf_op jit(solution)/shard_map/ppermute | solution.py:342
  59.8 20.9 %collective-permute-done.10 = bf16[128,2048]{1,0:T(8,128)(2,1)S(1)} collective-permute-done((bf16[128,2048]{1,0:T(8,128)(2,1)S(1)}, bf16[128,2048]{1,0:T(8,128)(2,1)S(1)}, u32[]{:S(2)}, u32[]{:S(2)}) %collective-permute-start.10) | collective-permute-done | bytes 524320 | tf_op jit(solution)/shard_map/ppermute | solution.py:347
  81.6 17.6 %collective-permute-done.12 = bf16[128,2048]{1,0:T(8,128)(2,1)S(1)} collective-permute-done((bf16[128,2048]{1,0:T(8,128)(2,1)S(1)}, bf16[128,2048]{1,0:T(8,128)(2,1)S(1)}, u32[]{:S(2)}, u32[]{:S(2)}) %collective-permute-start.12) | collective-permute-done | bytes 524320 | tf_op jit(solution)/shard_map/ppermute | solution.py:342
  102.1 32.1 %collective-permute-done.14 = bf16[128,2048]{1,0:T(8,128)(2,1)} collective-permute-done((bf16[128,2048]{1,0:T(8,128)(2,1)S(1)}, bf16[128,2048]{1,0:T(8,128)(2,1)}, u32[]{:S(2)}, u32[]{:S(2)}) %collective-permute-start.14) | collective-permute-done | bytes 524320 | tf_op jit(solution)/shard_map/ppermute | solution.py:342
  156.6 8.4 %collective-permute-done.4 = bf16[512,1024]{1,0:T(8,128)(2,1)} collective-permute-done((bf16[512,1024]{1,0:T(8,128)(2,1)S(1)}, bf16[512,1024]{1,0:T(8,128)(2,1)}, u32[]{:S(2)}, u32[]{:S(2)}) %collective-permute-start.4) | collective-permute-done | bytes 1048608 | tf_op jit(solution)/shard_map/ppermute | solution.py:309
  167.1 6.1 %collective-permute-done.17 = bf16[128,2048]{1,0:T(8,128)(2,1)} collective-permute-done((bf16[128,2048]{1,0:T(8,128)(2,1)}, bf16[128,2048]{1,0:T(8,128)(2,1)}, u32[]{:S(2)}, u32[]{:S(2)}) %collective-permute-start.17) | collective-permute-done | bytes 524320 | tf_op jit(solution)/shard_map/ppermute | solution.py:309
  192.4 15.2 %all-to-all-start.2 = ((bf16[8,128,160]{1,2,0:T(8,128)(2,1)}), bf16[8,128,160]{1,2,0:T(8,128)(2,1)S(1)}, u32[]{:S(2)}, u32[]{:S(2)}) async-start(bf16[8,128,160]{1,2,0:T(8,128)(2,1)} %copy_bitcast_fusion.4), calls=%async_computation.2 | async-start | bytes 655360 | tf_op jit(solution)/shard_map/all_to_all | solution.py:444
  207.6 5.9 %fusion.31 = f32[1024,512]{1,0:T(8,128)} fusion(bf16[512,2048]{1,0:T(8,128)(2,1)S(1)} %constant_dynamic-update-slice_fusion, bf16[1024,2048]{1,0:T(8,128)(2,1)} %select_dynamic-update-slice_fusion, pred[1024]{0:T(1024)(128)(4,1)} %iota_compare_fusion), kind=kOutput, calls=%fused_computation.65 | convolution fusion | flops 2149580800 | bytes 8389632 | tf_op jit(solution)/shard_map/dot_general | solution.py:459
  213.4 5.0 %all-to-all-done.2 = bf16[8,128,160]{1,2,0:T(8,128)(2,1)S(1)} async-done(((bf16[8,128,160]{1,2,0:T(8,128)(2,1)}), bf16[8,128,160]{1,2,0:T(8,128)(2,1)S(1)}, u32[]{:S(2)}, u32[]{:S(2)}) %all-to-all-start.2) | async-done | bytes 327712 | tf_op jit(solution)/shard_map/all_to_all | solution.py:444
  223.0 6.3 %fusion.35 = bf16[1024,512]{1,0:T(8,128)(2,1)} fusion(bf16[2048,1024]{1,0:T(8,128)(2,1)} %constant_dynamic-update-slice_fusion.12, bf16[1,1024,2048]{2,1,0:T(8,128)(2,1)} %all-gather.3.cloned.1.call-done, f32[2048]{0:T(1024)S(1)} %reshape.115, f32[1024]{0:T(1024)} %copy-done.46), kind=kOutput, calls=%fused_computation.67 | convolution fusion | flops 2156396544 | bytes 7352320 | tf_op jit(solution)/shard_map/dot_general | solution.py:459
  229.2 5.6 %all-to-all-done.3 = bf16[8,128,192]{1,2,0:T(8,128)(2,1)S(1)} async-done(((bf16[8,128,192]{1,2,0:T(8,128)(2,1)}), bf16[8,128,192]{1,2,0:T(8,128)(2,1)S(1)}, u32[]{:S(2)}, u32[]{:S(2)}) %all-to-all-start.3) | async-done | bytes 393248 | tf_op jit(solution)/shard_map/all_to_all | solution.py:455
  239.1 16.4 %scan_forward.1 = (f32[1024,512]{1,0:T(8,128)S(1)}, bf16[16384,512]{1,0:T(8,128)(2,1)}) custom-call(f32[1024,512]{1,0:T(8,128)S(1)} %get-tuple-element.140.delta, bf16[1024,512]{1,0:T(8,128)(2,1)S(1)} %multiply_convert_fusion.1.active, bf16[1024,192]{1,0:T(8,128)(2,1)S(1)} %bitcast.101, f32[16,512]{1,0:T(8,128)S(1)} %get-tuple-element.128.rate), custom_call_target="tpu_custom_call" | custom-call | flops 67108864 | bytes 22020096 | tf_op jit(solution)/shard_map/scan_forward/pallas_call | solution.py:90
  263.2 6.8 %fusion.8 = (f32[512]{0:T(512)}, f32[1024,512]{1,0:T(8,128)}, bf16[1024,512]{1,0:T(8,128)(2,1)S(1)}) fusion(f32[1024,512]{1,0:T(8,128)} %fusion.31, bf16[1024,512]{1,0:T(8,128)(2,1)} %fusion.35, f32[1024,512]{1,0:T(8,128)S(1)} %get-tuple-element.61, f32[512]{0:T(512)} %bitcast.143, bf16[1024,512]{1,0:T(8,128)(2,1)} %copy-done.4, f32[512]{0:T(512)S(1)} %bitcast.125, ...), kind=kLoop, calls=%fused_computation.33 | loop fusion | flops 18349568 | bytes 9451520 | tf_op jit(solution)/shard_map/reduce_sum | solution.py:568
  274.4 31.0 %scan_backward.1 = (f32[1024,512]{1,0:T(8,128)S(1)}, f32[1024,512]{1,0:T(8,128)}, f32[1024,32]{1,0:T(8,128)S(1)}, f32[16,512]{1,0:T(8,128)S(1)}) custom-call(f32[1024,512]{1,0:T(8,128)} %copy-done.3, bf16[1024,512]{1,0:T(8,128)(2,1)S(1)} %multiply_convert_fusion.1.active, f32[1024,512]{1,0:T(8,128)} %get-tuple-element.104.d_mixed, ...), custom_call_target="tpu_custom_call" | custom-call | flops 167772160 | bytes 27262976 | tf_op jit(solution)/shard_map/scan_backward/pallas_call | solution.py:251
  315.9 8.0 %all-to-all-done.4 = bf16[8,128,160]{1,2,0:T(8,128)(2,1)S(1)} async-done(((bf16[8,128,160]{1,2,0:T(8,128)(2,1)}), bf16[8,128,160]{1,2,0:T(8,128)(2,1)S(1)}, u32[]{:S(2)}, u32[]{:S(2)}) %all-to-all-start.4) | async-done | bytes 327712 | tf_op jit(solution)/shard_map/all_to_all | solution.py:444
  332.6 12.1 %all-to-all-done.5 = bf16[8,128,160]{1,2,0:T(8,128)(2,1)S(1)} async-done(((bf16[8,128,160]{1,2,0:T(8,128)(2,1)}), bf16[8,128,160]{1,2,0:T(8,128)(2,1)S(1)}, u32[]{:S(2)}, u32[]{:S(2)}) %all-to-all-start.5) | async-done | bytes 327712 | tf_op jit(solution)/shard_map/all_to_all | solution.py:455
  361.0 9.0 %convolution_convert_fusion.1 = bf16[1024,2048]{1,0:T(8,128)(2,1)} fusion(bf16[2048,1024]{1,0:T(8,128)(2,1)} %constant_dynamic-update-slice_fusion.12, bf16[1024,512]{1,0:T(8,128)(2,1)S(1)} %copy-done.31, bf16[1024,512]{1,0:T(8,128)(2,1)} %copy-done.29), kind=kOutput, calls=%fused_computation.14 | convolution fusion | flops 4301258752 | bytes 10485760 | tf_op jit(solution)/shard_map/dot_general | solution.py:459
  373.6 7.0 %collective-permute-start.22 = (bf16[128,2048]{1,0:T(8,128)(2,1)}, bf16[128,2048]{1,0:T(8,128)(2,1)}, u32[]{:S(2)}, u32[]{:S(2)}) collective-permute-start(bf16[128,2048]{1,0:T(8,128)(2,1)} %get-tuple-element.118), channel_id=1, source_target_pairs={{0,1},{1,0},{6,7},{7,6},{8,9},{9,8},{14,15},{15,14},{16,17},{17,16... | collective-permute-start | bytes 1572872 | tf_op jit(solution)/shard_map/ppermute | solution.py:347
  397.6 6.1 %convolution_convert_fusion.2 = bf16[512,2048]{1,0:T(8,128)(2,1)} fusion(bf16[1024,512]{1,0:T(8,128)(2,1)S(1)} %copy-done.28, bf16[1024,2048]{1,0:T(8,128)(2,1)} %select_dynamic-update-slice_fusion, pred[1024]{0:T(1024)(128)(4,1)S(1)} %copy-done.50), kind=kOutput, calls=%fused_computation.19 | convolution fusion | flops 2150629376 | bytes 7341056 | tf_op jit(solution)/shard_map/dot_general | solution.py:459
  406.5 8.9 %collective-permute-done.25 = bf16[128,2048]{1,0:T(8,128)(2,1)} collective-permute-done((bf16[128,2048]{1,0:T(8,128)(2,1)}, bf16[128,2048]{1,0:T(8,128)(2,1)}, u32[]{:S(2)}, u32[]{:S(2)}) %collective-permute-start.25) | collective-permute-done | bytes 524320 | tf_op jit(solution)/shard_map/ppermute | solution.py:347
  419.6 5.8 %collective-permute-start.27 = (bf16[128,2048]{1,0:T(8,128)(2,1)}, bf16[128,2048]{1,0:T(8,128)(2,1)}, u32[]{:S(2)}, u32[]{:S(2)}) collective-permute-start(bf16[128,2048]{1,0:T(8,128)(2,1)} %add_convert_fusion.4), channel_id=1, source_target_pairs={{0,2},{1,3},{2,4},{3,5},{8,10},{9,11},{10,12},{11,13},{16,18},{17,... | collective-permute-start | bytes 1572872 | tf_op jit(solution)/shard_map/ppermute | solution.py:342
  446.3 6.5 %collective-permute-start.33 = (bf16[128,2048]{1,0:T(8,128)(2,1)}, bf16[128,2048]{1,0:T(8,128)(2,1)S(1)}, u32[]{:S(2)}, u32[]{:S(2)}) collective-permute-start(bf16[128,2048]{1,0:T(8,128)(2,1)} %get-tuple-element.111), channel_id=1, source_target_pairs={{0,2},{1,3},{2,4},{3,5},{4,6},{5,7},{8,10},{9,11},{10,12},{11,13},... | collective-permute-start | bytes 1572872 | tf_op jit(solution)/shard_map/ppermute | solution.py:342
  (285 shorter events, 192.1 us)
Async XLA Ops:
  7.2 174.1 %all-gather.3.cloned.1.call-start = ((), (), s32[]{:S(2)}) async-start(), calls=%async_computation.14 | async-start | bytes 4718592 | tf_op jit(solution)/shard_map/all_gather | solution.py:525
  14.6 41.8 %collective-permute-start.6 = (bf16[128,2048]{1,0:T(8,128)(2,1)}, bf16[128,2048]{1,0:T(8,128)(2,1)S(1)}, u32[]{:S(2)}, u32[]{:S(2)}) collective-permute-start(bf16[128,2048]{1,0:T(8,128)(2,1)} %bitcast.110), channel_id=1, source_target_pairs={{0,1},{1,0},{2,3},{3,2},{4,5},{5,4},{6,7},{7,6},{8,9},{9,8},{10,11... | collective-permute-start | bytes 1572872 | tf_op jit(solution)/shard_map/ppermute | solution.py:347
  16.1 26.5 %collective-permute-start.7 = (bf16[128,2048]{1,0:T(8,128)(2,1)}, bf16[128,2048]{1,0:T(8,128)(2,1)S(1)}, u32[]{:S(2)}, u32[]{:S(2)}) collective-permute-start(bf16[128,2048]{1,0:T(8,128)(2,1)} %bitcast.111), channel_id=1, source_target_pairs={{0,2},{1,3},{2,4},{3,5},{4,6},{5,7},{8,10},{9,11},{10,12},{11,13},... | collective-permute-start | bytes 1572872 | tf_op jit(solution)/shard_map/ppermute | solution.py:342
  19.6 32.7 %collective-permute-start.8 = (bf16[128,2048]{1,0:T(8,128)(2,1)}, bf16[128,2048]{1,0:T(8,128)(2,1)S(1)}, u32[]{:S(2)}, u32[]{:S(2)}) collective-permute-start(bf16[128,2048]{1,0:T(8,128)(2,1)} %bitcast.112), channel_id=1, source_target_pairs={{2,0},{3,1},{4,2},{5,3},{6,4},{7,5},{10,8},{11,9},{12,10},{13,11},... | collective-permute-start | bytes 1572872 | tf_op jit(solution)/shard_map/ppermute | solution.py:342
  24.4 114.3 %all-to-all-start = ((bf16[8,64,1024]{2,1,0:T(8,128)(2,1)}), bf16[8,64,1024]{2,1,0:T(8,128)(2,1)S(1)}, u32[]{:S(2)}, u32[]{:S(2)}) async-start(bf16[8,64,1024]{2,1,0:T(8,128)(2,1)} %reshape.106), calls=%async_computation | async-start | bytes 2097152 | tf_op jit(solution)/shard_map/all_to_all | solution.py:492
  43.3 38.2 %collective-permute-start.11 = (bf16[128,2048]{1,0:T(8,128)(2,1)S(1)}, bf16[128,2048]{1,0:T(8,128)(2,1)S(1)}, u32[]{:S(2)}, u32[]{:S(2)}) collective-permute-start(bf16[128,2048]{1,0:T(8,128)(2,1)S(1)} %collective-permute-done.7), channel_id=1, source_target_pairs={{2,4},{3,5},{4,6},{5,7},{10,12},{11,13},{12,14},{13,15},{18,20},{1... | collective-permute-start | bytes 1572872 | tf_op jit(solution)/shard_map/ppermute | solution.py:342
  52.3 28.4 %collective-permute-start.10 = (bf16[128,2048]{1,0:T(8,128)(2,1)S(1)}, bf16[128,2048]{1,0:T(8,128)(2,1)S(1)}, u32[]{:S(2)}, u32[]{:S(2)}) collective-permute-start(bf16[128,2048]{1,0:T(8,128)(2,1)S(1)} %collective-permute-done.8), channel_id=1, source_target_pairs={{0,1},{1,0},{2,3},{3,2},{4,5},{5,4},{8,9},{9,8},{10,11},{11,10},{1... | collective-permute-start | bytes 1572872 | tf_op jit(solution)/shard_map/ppermute | solution.py:347
  55.2 44.0 %collective-permute-start.12 = (bf16[128,2048]{1,0:T(8,128)(2,1)S(1)}, bf16[128,2048]{1,0:T(8,128)(2,1)S(1)}, u32[]{:S(2)}, u32[]{:S(2)}) collective-permute-start(bf16[128,2048]{1,0:T(8,128)(2,1)S(1)} %collective-permute-done.8), channel_id=1, source_target_pairs={{2,0},{3,1},{4,2},{5,3},{10,8},{11,9},{12,10},{13,11},{18,16},{19,... | collective-permute-start | bytes 1572872 | tf_op jit(solution)/shard_map/ppermute | solution.py:342
  100.1 37.8 %collective-permute-start.13 = (bf16[128,2048]{1,0:T(8,128)(2,1)S(1)}, bf16[128,2048]{1,0:T(8,128)(2,1)S(1)}, u32[]{:S(2)}, u32[]{:S(2)}) collective-permute-start(bf16[128,2048]{1,0:T(8,128)(2,1)S(1)} %get-tuple-element.110), channel_id=1, source_target_pairs={{0,1},{1,0},{2,3},{3,2},{4,5},{5,4},{6,7},{7,6},{8,9},{9,8},{10,11... | collective-permute-start | bytes 1572872 | tf_op jit(solution)/shard_map/ppermute | solution.py:347
  100.1 34.1 %collective-permute-start.14 = (bf16[128,2048]{1,0:T(8,128)(2,1)S(1)}, bf16[128,2048]{1,0:T(8,128)(2,1)}, u32[]{:S(2)}, u32[]{:S(2)}) collective-permute-start(bf16[128,2048]{1,0:T(8,128)(2,1)S(1)} %get-tuple-element.110), channel_id=1, source_target_pairs={{4,6},{5,7},{2,0},{3,1},{12,14},{13,15},{10,8},{11,9},{20,22},{21,... | collective-permute-start | bytes 1572872 | tf_op jit(solution)/shard_map/ppermute | solution.py:342
  134.2 30.7 %collective-permute-start.15 = (bf16[128,2048]{1,0:T(8,128)(2,1)}, bf16[128,2048]{1,0:T(8,128)(2,1)}, u32[]{:S(2)}, u32[]{:S(2)}) collective-permute-start(bf16[128,2048]{1,0:T(8,128)(2,1)} %collective-permute-done.14), channel_id=1, source_target_pairs={{0,1},{1,0},{6,7},{7,6},{8,9},{9,8},{14,15},{15,14},{16,17},{17,16... | collective-permute-start | bytes 1572872 | tf_op jit(solution)/shard_map/ppermute | solution.py:347
  138.8 26.2 %collective-permute-start.4 = (bf16[512,1024]{1,0:T(8,128)(2,1)S(1)}, bf16[512,1024]{1,0:T(8,128)(2,1)}, u32[]{:S(2)}, u32[]{:S(2)}) collective-permute-start(bf16[512,1024]{1,0:T(8,128)(2,1)S(1)} %bitcast.105), channel_id=1, source_target_pairs={{0,16},{8,24},{16,0},{24,8},{1,17},{9,25},{17,1},{25,9},{2,18},{10... | collective-permute-start | bytes 3145736 | tf_op jit(solution)/shard_map/ppermute | solution.py:309
  140.9 34.5 %collective-permute-start.3 = (bf16[512,1024]{1,0:T(8,128)(2,1)S(1)}, bf16[512,1024]{1,0:T(8,128)(2,1)}, u32[]{:S(2)}, u32[]{:S(2)}) collective-permute-start(bf16[512,1024]{1,0:T(8,128)(2,1)S(1)} %bitcast.106), channel_id=1, source_target_pairs={{0,8},{8,0},{16,24},{24,16},{1,9},{9,1},{17,25},{25,17},{2,10},{10... | collective-permute-start | bytes 3145736 | tf_op jit(solution)/shard_map/ppermute | solution.py:302
  140.9 32.4 %collective-permute-start.16 = (bf16[128,2048]{1,0:T(8,128)(2,1)}, bf16[128,2048]{1,0:T(8,128)(2,1)}, u32[]{:S(2)}, u32[]{:S(2)}) collective-permute-start(bf16[128,2048]{1,0:T(8,128)(2,1)} %param.24), channel_id=1, source_target_pairs={{0,8},{8,0},{16,24},{24,16},{1,9},{9,1},{17,25},{25,17},{2,10},{10... | collective-permute-start | bytes 1572872 | tf_op jit(solution)/shard_map/ppermute | solution.py:302
  141.4 31.8 %collective-permute-start.17 = (bf16[128,2048]{1,0:T(8,128)(2,1)}, bf16[128,2048]{1,0:T(8,128)(2,1)}, u32[]{:S(2)}, u32[]{:S(2)}) collective-permute-start(bf16[128,2048]{1,0:T(8,128)(2,1)} %param.24), channel_id=1, source_target_pairs={{0,16},{8,24},{16,0},{24,8},{1,17},{9,25},{17,1},{25,9},{2,18},{10... | collective-permute-start | bytes 1572872 | tf_op jit(solution)/shard_map/ppermute | solution.py:309
  192.4 26.0 %all-to-all-start.2 = ((bf16[8,128,160]{1,2,0:T(8,128)(2,1)}), bf16[8,128,160]{1,2,0:T(8,128)(2,1)S(1)}, u32[]{:S(2)}, u32[]{:S(2)}) async-start(bf16[8,128,160]{1,2,0:T(8,128)(2,1)} %copy_bitcast_fusion.4), calls=%async_computation.2 | async-start | bytes 655360 | tf_op jit(solution)/shard_map/all_to_all | solution.py:444
  222.9 138.1 %reduce-scatter.4.cloned.1.call-start = ((), (), s32[]{:S(2)}) async-start(), calls=%async_computation.11 | async-start | bytes 4718592 | tf_op jit(solution)/shard_map/reduce_scatter | solution.py:562
  273.8 39.7 %collective-permute-start.19 = (bf16[512,512]{1,0:T(8,128)(2,1)}, bf16[512,512]{1,0:T(8,128)(2,1)}, u32[]{:S(2)}, u32[]{:S(2)}) collective-permute-start(bf16[512,512]{1,0:T(8,128)(2,1)} %get-tuple-element.122), channel_id=1, source_target_pairs={{0,8},{8,0},{16,24},{24,16},{1,9},{9,1},{17,25},{25,17},{2,10},{10... | collective-permute-start | bytes 1572872 | tf_op jit(solution)/shard_map/ppermute | solution.py:302
  349.1 83.6 %reduce-scatter.6.cloned.1.call-start = ((), (), s32[]{:S(2)}) async-start(), calls=%async_computation.12 | async-start | bytes 798720 | tf_op jit(solution)/shard_map/reduce_scatter | solution.py:632
  385.7 71.8 %reduce-scatter.8.cloned.1.call-start = ((), (), s32[]{:S(2)}) async-start(), calls=%async_computation.13 | async-start | bytes 2621440 | tf_op jit(solution)/shard_map/reduce_scatter | solution.py:613
  385.8 29.6 %collective-permute-start.25 = (bf16[128,2048]{1,0:T(8,128)(2,1)}, bf16[128,2048]{1,0:T(8,128)(2,1)}, u32[]{:S(2)}, u32[]{:S(2)}) collective-permute-start(bf16[128,2048]{1,0:T(8,128)(2,1)} %get-tuple-element.116), channel_id=1, source_target_pairs={{0,1},{1,0},{2,3},{3,2},{4,5},{5,4},{8,9},{9,8},{10,11},{11,10},{1... | collective-permute-start | bytes 1572872 | tf_op jit(solution)/shard_map/ppermute | solution.py:347
  389.8 27.4 %collective-permute-start.26 = (bf16[128,2048]{1,0:T(8,128)(2,1)}, bf16[128,2048]{1,0:T(8,128)(2,1)}, u32[]{:S(2)}, u32[]{:S(2)}) collective-permute-start(bf16[128,2048]{1,0:T(8,128)(2,1)} %get-tuple-element.115), channel_id=1, source_target_pairs={{2,3},{3,2},{4,5},{5,4},{6,7},{7,6},{10,11},{11,10},{12,13},{13,12... | collective-permute-start | bytes 1572872 | tf_op jit(solution)/shard_map/ppermute | solution.py:347
  415.4 25.7 %collective-permute-start.29 = (bf16[128,2048]{1,0:T(8,128)(2,1)}, bf16[128,2048]{1,0:T(8,128)(2,1)}, u32[]{:S(2)}, u32[]{:S(2)}) collective-permute-start(bf16[128,2048]{1,0:T(8,128)(2,1)} %get-tuple-element.114), channel_id=1, source_target_pairs={{0,1},{1,0},{2,3},{3,2},{4,5},{5,4},{6,7},{7,6},{8,9},{9,8},{10,11... | collective-permute-start | bytes 1572872 | tf_op jit(solution)/shard_map/ppermute | solution.py:347
  427.8 25.0 %all-to-all-start.7 = ((bf16[8,64,512]{2,1,0:T(8,128)(2,1)}), bf16[8,64,512]{2,1,0:T(8,128)(2,1)S(1)}, u32[]{:S(2)}, u32[]{:S(2)}) async-start(bf16[8,64,512]{2,1,0:T(8,128)(2,1)} %bitcast.34), calls=%async_computation.9 | async-start | bytes 1048576 | tf_op jit(solution)/shard_map/all_to_all | solution.py:625
  (74 other events, 1174.9 us)
Sparse Core Ops, SparseCore 0:
  10.1 111.0 all-gather.2
  263.3 97.2 reduce-scatter.3
  385.8 18.8 reduce-scatter.5
  407.2 32.0 reduce-scatter.7

commit v4 on v1

--- a/solution.py
+++ b/solution.py
@@ -493,6 +493,11 @@
     halves = in_proj.reshape(in_rows, 2, batch, seq, own).transpose(1, 3, 0, 2, 4)
     halves = halves.reshape(2, seq, in_rows, width)
     columns = lax.all_to_all(halves[0], "seq", 0, 0)
+    columns, gate_columns = together((columns, halves[1]))
+    gate_columns = lax.all_to_all(gate_columns, "seq", 0, 0)
+    upstream, (dt_proj, x_proj, out_proj) = line_gathered(
+        cotangent[0], "seq", (dt_proj, x_proj, out_proj)
+    )
     small = jnp.concatenate(
         [
             dt_proj,
@@ -516,11 +521,8 @@
     delta_shift, skip_gain = delta_shift.astype(f32), skip_gain.astype(f32)
     decay = -jnp.exp(decay_logs.astype(f32))
     gain = gain.reshape(batch, own)[:, :in_rows]
-    columns, gain = together((columns, gain))
-    gain = shared(gain, "seq")
-    gate_columns, gain = together((halves[1], gain))
-    gate_columns = lax.all_to_all(gate_columns, "seq", 0, 0)
-    gain = gain.transpose(1, 0, 2).reshape(model).astype(f32)
+    gate_columns, gain = together((gate_columns, gain))
+    gain = shared(gain, "seq").transpose(1, 0, 2).reshape(model).astype(f32)
 
     input_weight = gathered(columns.reshape(seq * in_rows, width), "batch")
 
@@ -530,9 +532,7 @@
         return (rows * scale * gain).astype(bf16)
 
     stream = lax.all_gather(tokens[0], "seq", axis=0, tiled=True)
-    gate_weight = gathered(gate_columns.reshape(seq * in_rows, width), "batch")
     normalized = normed(stream)
-    upstream, out_proj = line_gathered(cotangent[0], "seq", out_proj)
     output_weight = gathered(out_proj, "batch")
 
     valid = (jnp.arange(length, dtype=jnp.int32) < lengths[0])[:, None]
@@ -544,7 +544,10 @@
     active = jax.nn.silu(conv_out).astype(bf16)
     active_f = active.astype(f32)
 
-    partial, upstream = together((matmul(active, select_weight, NT), upstream))
+    partial, upstream, gate_columns = together(
+        (matmul(active, select_weight, NT), upstream, gate_columns)
+    )
+    gate_weight = gathered(gate_columns.reshape(seq * in_rows, width), "batch")
     select = summed_over_seq(
         partial,
         lambda s: jnp.concatenate([s[:, :rank].astype(bf16)] + two_terms(s[:, rank:]), axis=1),

time: 457 us -> 445 us (0.974)
  local copies, waits for them, and re-layouts: 68.9 us -> 62.1 us
  waiting for transfers between devices: 115 us -> 109 us
    ppermute x10, waiting for transfers between devices: 16.2 us -> 57.4 us  [hop(): return lax.ppermute(value, axis, pairs)]
    all_to_all x3, waiting for transfers between devices: 40.6 us -> 20.5 us  [shared(): return lax.all_to_all(wide, axis, 0, 0)]
    all_to_all x3, starting transfers between devices: 28.6 us -> 12.1 us  [shared(): return lax.all_to_all(wide, axis, 0, 0)]
    ppermute x6, waiting for transfers between devices: 17.2 us -> 3.62 us  [outer_shift(): return lax.ppermute(value, axis, pairs)]
    ppermute x10, waiting for transfers between devices: 28.9 us -> 16.3 us  [swap_at(): return lax.ppermute(value, axis, pairs)]
    all_to_all x2, starting transfers between devices: 11 us -> 19 us  [summed_over_seq(): own = change(jnp.sum(lax.all_to_all(part, 'seq', 0, 0).astype(f32), axis=0))]
    unnamed x94 -> x113, local copies, waits for them, and re-layouts: 6.87 us -> 9.23 us
  transfers between devices with their start and end apart: 51 -> 51, of which waited for: 18 -> 16; matrix products, arithmetic and copies ran while one was open for 33% -> 31% of each run, Pallas kernels for 7% -> 7%
where the time goes in v4:
time: 445 us; the launch traced here: 440 us
  waiting for transfers between devices  109 us (24%)
  starting transfers between devices  105 us (24%)
  local copies, waits for them, and re-layouts  62.1 us (14%)
  matrix products  54.1 us (12%)
  Pallas kernels  47.5 us (11%)
  other arithmetic  46.6 us (10%)
  between operations  15.8 us (4%)
    ppermute x10, waiting for transfers between devices, hop(): return lax.ppermute(value, axis, pairs)  57.4 us
    dot_general x14, matrix products, matmul(): return lax.dot_general(a, b, dims, preferred_element_type=f32)  54.1 us
    pallas_call x1, Pallas kernels, scan_backward(): pl.pallas_call(functools.partial(backward_body, tiles, step), grid=(block...  31 us
    ppermute x10, starting transfers between devices, hop(): return lax.ppermute(value, axis, pairs)  24.9 us
    ppermute x10, starting transfers between devices, swap_at(): return lax.ppermute(value, axis, pairs)  21.5 us
    all_to_all x3, waiting for transfers between devices, shared(): return lax.all_to_all(wide, axis, 0, 0)  20.5 us
    all_to_all x2, starting transfers between devices, summed_over_seq(): own = change(jnp.sum(lax.all_to_all(part, 'seq', 0, 0).astype(f32), axis=0))  19 us
    pallas_call x1, Pallas kernels, scan_forward(): pl.pallas_call(functools.partial(forward_body, tiles, step), grid=(length...  16.4 us
  transfers between devices with their start and end apart: 51, of which 16 were waited for; matrix products, arithmetic and copies ran while one was open for 31% of the time, Pallas kernels for 7%

profile of v4, /device:TPU:0, one launch (start us, length us, event | category | flops | bytes accessed | tf_op | source)
XLA Modules:
  0.0 439.6 jit_solution(8762744903409457269)
XLA Ops:
  7.9 5.8 %collective-permute-start = (bf16[128,2048]{1,0:T(8,128)(2,1)}, bf16[128,2048]{1,0:T(8,128)(2,1)}, u32[]{:S(2)}, u32[]{:S(2)}) collective-permute-start(bf16[128,2048]{1,0:T(8,128)(2,1)} %bitcast.115), channel_id=1, source_target_pairs={{0,2},{1,3},{2,4},{3,5},{4,6},{5,7},{8,10},{9,11},{10,12},{11,13},... | collective-permute-start | bytes 1572872 | tf_op jit(solution)/shard_map/ppermute | solution.py:342
  20.0 5.9 %all-to-all-start = ((bf16[8,64,512]{2,1,0:T(8,128)(2,1)}), bf16[8,64,512]{2,1,0:T(8,128)(2,1)S(1)}, u32[]{:S(2)}, u32[]{:S(2)}) async-start(bf16[8,64,512]{2,1,0:T(8,128)(2,1)} %squeeze.29), calls=%async_computation | async-start | bytes 1048576 | tf_op jit(solution)/shard_map/all_to_all | solution.py:495
  31.6 14.6 %collective-permute-done.1 = bf16[128,2048]{1,0:T(8,128)(2,1)} collective-permute-done((bf16[128,2048]{1,0:T(8,128)(2,1)}, bf16[128,2048]{1,0:T(8,128)(2,1)}, u32[]{:S(2)}, u32[]{:S(2)}) %collective-permute-start.1) | collective-permute-done | bytes 524320 | tf_op jit(solution)/shard_map/ppermute | solution.py:342
  64.0 5.1 %all-to-all-start.1 = ((bf16[8,64,512]{2,1,0:T(8,128)(2,1)}), bf16[8,64,512]{2,1,0:T(8,128)(2,1)}, u32[]{:S(2)}, u32[]{:S(2)}) async-start(bf16[8,64,512]{2,1,0:T(8,128)(2,1)} %squeeze.30), calls=%async_computation.1 | async-start | bytes 1048576 | tf_op jit(solution)/shard_map/all_to_all | solution.py:497
  77.3 16.2 %collective-permute-done.12 = bf16[128,2048]{1,0:T(8,128)(2,1)} collective-permute-done((bf16[128,2048]{1,0:T(8,128)(2,1)}, bf16[128,2048]{1,0:T(8,128)(2,1)}, u32[]{:S(2)}, u32[]{:S(2)}) %collective-permute-start.12) | collective-permute-done | bytes 524320 | tf_op jit(solution)/shard_map/ppermute | solution.py:342
  103.4 26.6 %collective-permute-done.14 = bf16[128,2048]{1,0:T(8,128)(2,1)} collective-permute-done((bf16[128,2048]{1,0:T(8,128)(2,1)S(1)}, bf16[128,2048]{1,0:T(8,128)(2,1)}, u32[]{:S(2)}, u32[]{:S(2)}) %collective-permute-start.14) | collective-permute-done | bytes 524320 | tf_op jit(solution)/shard_map/ppermute | solution.py:342
  141.5 5.1 %all-to-all-done.2 = bf16[8,2,128]{2,1,0:T(2,128)(2,1)} async-done(((bf16[8,2,128]{2,1,0:T(2,128)(2,1)}), bf16[8,2,128]{2,1,0:T(2,128)(2,1)}, u32[]{:S(2)}, u32[]{:S(2)}) %all-to-all-start.2) | async-done | bytes 4128 | tf_op jit(solution)/shard_map/all_to_all | solution.py:457
  162.9 15.4 %all-to-all-start.3 = ((bf16[8,128,160]{1,2,0:T(8,128)(2,1)}), bf16[8,128,160]{1,2,0:T(8,128)(2,1)S(1)}, u32[]{:S(2)}, u32[]{:S(2)}) async-start(bf16[8,128,160]{1,2,0:T(8,128)(2,1)} %copy_bitcast_fusion.4), calls=%async_computation.3 | async-start | bytes 655360 | tf_op jit(solution)/shard_map/all_to_all | solution.py:446
  178.3 5.9 %fusion.34 = f32[1024,512]{1,0:T(8,128)} fusion(bf16[512,2048]{1,0:T(8,128)(2,1)S(1)} %constant_dynamic-update-slice_fusion, bf16[1024,2048]{1,0:T(8,128)(2,1)} %select_dynamic-update-slice_fusion, pred[1024]{0:T(1024)(128)(4,1)} %iota_compare_fusion), kind=kOutput, calls=%fused_computation.65 | convolution fusion | flops 2149580800 | bytes 8389632 | tf_op jit(solution)/shard_map/dot_general | solution.py:461
  189.7 4.6 %all-to-all-start.4 = ((bf16[8,128,192]{1,2,0:T(8,128)(2,1)}), bf16[8,128,192]{1,2,0:T(8,128)(2,1)}, u32[]{:S(2)}, u32[]{:S(2)}) async-start(bf16[8,128,192]{1,2,0:T(8,128)(2,1)} %broadcast_in_dim.96), calls=%async_computation.4 | async-start | bytes 786432 | tf_op jit(solution)/shard_map/all_to_all | solution.py:457
  195.5 6.3 %convolution_convert_fusion.4 = bf16[1024,512]{1,0:T(8,128)(2,1)} fusion(bf16[2048,512]{1,0:T(8,128)(2,1)S(1)} %constant_dynamic-update-slice_fusion.4, bf16[1,1024,2048]{2,1,0:T(8,128)(2,1)} %all-gather.3.cloned.1.call-done, f32[2048]{0:T(1024)S(1)} %reshape.120, f32[1024]{0:T(1024)} %copy-done.44), kind=kOutput, calls=%fused_computation.66 | convolution fusion | flops 2156396544 | bytes 7352320 | tf_op jit(solution)/shard_map/dot_general | solution.py:461
  201.8 4.9 %all-to-all-done.4 = bf16[8,128,192]{1,2,0:T(8,128)(2,1)} async-done(((bf16[8,128,192]{1,2,0:T(8,128)(2,1)}), bf16[8,128,192]{1,2,0:T(8,128)(2,1)}, u32[]{:S(2)}, u32[]{:S(2)}) %all-to-all-start.4) | async-done | bytes 393248 | tf_op jit(solution)/shard_map/all_to_all | solution.py:457
  211.9 16.4 %scan_forward.1 = (f32[1024,512]{1,0:T(8,128)S(1)}, bf16[16384,512]{1,0:T(8,128)(2,1)}) custom-call(f32[1024,512]{1,0:T(8,128)S(1)} %get-tuple-element.158.delta, bf16[1024,512]{1,0:T(8,128)(2,1)S(1)} %multiply_convert_fusion.1.active, bf16[1024,192]{1,0:T(8,128)(2,1)S(1)} %bitcast.105, f32[16,512]{1,0:T(8,128)S(1)} %get-tuple-element.146.rate), custom_call_target="tpu_custom_call" | custom-call | flops 67108864 | bytes 22020096 | tf_op jit(solution)/shard_map/scan_forward/pallas_call | solution.py:90
  231.6 4.4 convolution_convert_fusion
  236.1 6.7 %fusion.15 = (f32[512]{0:T(512)}, f32[1024,512]{1,0:T(8,128)}, bf16[1024,512]{1,0:T(8,128)(2,1)S(1)}) fusion(f32[1024,512]{1,0:T(8,128)} %fusion.34, bf16[1024,512]{1,0:T(8,128)(2,1)} %convolution_convert_fusion.4, f32[1024,512]{1,0:T(8,128)S(1)} %get-tuple-element.77, f32[512]{0:T(512)} %bitcast.151, bf16[1024,512]{1,0:T(8,128)(2,1)} %copy-done.4, ...), kind=kLoop, calls=%fused_computation.37 | loop fusion | flops 18349568 | bytes 9451520 | tf_op jit(solution)/shard_map/reduce_sum | solution.py:579
  247.1 31.0 %scan_backward.1 = (f32[1024,512]{1,0:T(8,128)S(1)}, f32[1024,512]{1,0:T(8,128)}, f32[1024,32]{1,0:T(8,128)S(1)}, f32[16,512]{1,0:T(8,128)S(1)}) custom-call(f32[1024,512]{1,0:T(8,128)} %copy-done.3, bf16[1024,512]{1,0:T(8,128)(2,1)S(1)} %multiply_convert_fusion.1.active, f32[1024,512]{1,0:T(8,128)} %get-tuple-element.120.d_mixed, ...), custom_call_target="tpu_custom_call" | custom-call | flops 167772160 | bytes 27262976 | tf_op jit(solution)/shard_map/scan_backward/pallas_call | solution.py:251
  290.0 6.6 %all-to-all-done.5 = bf16[8,128,160]{1,2,0:T(8,128)(2,1)S(1)} async-done(((bf16[8,128,160]{1,2,0:T(8,128)(2,1)}), bf16[8,128,160]{1,2,0:T(8,128)(2,1)S(1)}, u32[]{:S(2)}, u32[]{:S(2)}) %all-to-all-start.5) | async-done | bytes 327712 | tf_op jit(solution)/shard_map/all_to_all | solution.py:446
  305.3 10.4 %all-to-all-done.6 = bf16[8,128,160]{1,2,0:T(8,128)(2,1)S(1)} async-done(((bf16[8,128,160]{1,2,0:T(8,128)(2,1)}), bf16[8,128,160]{1,2,0:T(8,128)(2,1)S(1)}, u32[]{:S(2)}, u32[]{:S(2)}) %all-to-all-start.6) | async-done | bytes 327712 | tf_op jit(solution)/shard_map/all_to_all | solution.py:457
  330.0 6.7 %convolution_convert_fusion.2 = bf16[2048,512]{1,0:T(8,128)(2,1)} fusion(bf16[1024,512]{1,0:T(8,128)(2,1)} %get-tuple-element.87, bf16[1,1024,2048]{2,1,0:T(8,128)(2,1)} %all-gather.3.cloned.1.call-done, f32[2048]{0:T(1024)S(1)} %reshape.120, f32[1024]{0:T(1024)S(1)} %copy-done.46), kind=kOutput, calls=%fused_computation.24 | convolution fusion | flops 2156920832 | bytes 7352320 | tf_op jit(solution)/shard_map/dot_general | solution.py:461
  338.0 8.8 %fusion.7 = bf16[1024,2048]{1,0:T(8,128)(2,1)} fusion(bf16[2048,512]{1,0:T(8,128)(2,1)S(1)} %copy-done.15, bf16[2048,512]{1,0:T(8,128)(2,1)} %constant_dynamic-update-slice_fusion.16, bf16[1024,512]{1,0:T(8,128)(2,1)} %copy-done.26, bf16[1024,512]{1,0:T(8,128)(2,1)} %get-tuple-element.87), kind=kOutput, calls=%fused_computation.17 | convolution fusion | flops 4309647360 | bytes 10485760 | tf_op jit(solution)/shard_map/dot_general | solution.py:461
  359.1 6.0 %convolution_convert_fusion.1 = bf16[512,2048]{1,0:T(8,128)(2,1)} fusion(bf16[1024,512]{1,0:T(8,128)(2,1)S(1)} %copy-done.25, bf16[1024,2048]{1,0:T(8,128)(2,1)} %select_dynamic-update-slice_fusion, pred[1024]{0:T(1024)(128)(4,1)S(1)} %copy-done.53), kind=kOutput, calls=%fused_computation.23 | convolution fusion | flops 2150629376 | bytes 7341056 | tf_op jit(solution)/shard_map/dot_general | solution.py:461
  371.2 7.1 %collective-permute-done.27 = bf16[128,2048]{1,0:T(8,128)(2,1)} collective-permute-done((bf16[128,2048]{1,0:T(8,128)(2,1)}, bf16[128,2048]{1,0:T(8,128)(2,1)}, u32[]{:S(2)}, u32[]{:S(2)}) %collective-permute-start.27) | collective-permute-done | bytes 524320 | tf_op jit(solution)/shard_map/ppermute | solution.py:347
  379.8 8.9 %collective-permute-done.28 = bf16[128,2048]{1,0:T(8,128)(2,1)} collective-permute-done((bf16[128,2048]{1,0:T(8,128)(2,1)}, bf16[128,2048]{1,0:T(8,128)(2,1)}, u32[]{:S(2)}, u32[]{:S(2)}) %collective-permute-start.28) | collective-permute-done | bytes 524320 | tf_op jit(solution)/shard_map/ppermute | solution.py:347
  416.8 6.2 %collective-permute-start.36 = (bf16[128,2048]{1,0:T(8,128)(2,1)}, bf16[128,2048]{1,0:T(8,128)(2,1)S(1)}, u32[]{:S(2)}, u32[]{:S(2)}) collective-permute-start(bf16[128,2048]{1,0:T(8,128)(2,1)} %get-tuple-element.127), channel_id=1, source_target_pairs={{0,2},{1,3},{2,4},{3,5},{4,6},{5,7},{8,10},{9,11},{10,12},{11,13},... | collective-permute-start | bytes 1572872 | tf_op jit(solution)/shard_map/ppermute | solution.py:342
  (306 shorter events, 188.1 us)
Async XLA Ops:
  7.2 144.1 %all-gather.3.cloned.1.call-start = ((), (), s32[]{:S(2)}) async-start(), calls=%async_computation.15 | async-start | bytes 4718592 | tf_op jit(solution)/shard_map/all_gather | solution.py:534
  13.7 32.4 %collective-permute-start.1 = (bf16[128,2048]{1,0:T(8,128)(2,1)}, bf16[128,2048]{1,0:T(8,128)(2,1)}, u32[]{:S(2)}, u32[]{:S(2)}) collective-permute-start(bf16[128,2048]{1,0:T(8,128)(2,1)} %bitcast.116), channel_id=1, source_target_pairs={{2,0},{3,1},{4,2},{5,3},{6,4},{7,5},{10,8},{11,9},{12,10},{13,11},... | collective-permute-start | bytes 1572872 | tf_op jit(solution)/shard_map/ppermute | solution.py:342
  15.0 31.2 %collective-permute-start.2 = (bf16[128,2048]{1,0:T(8,128)(2,1)}, bf16[128,2048]{1,0:T(8,128)(2,1)S(1)}, u32[]{:S(2)}, u32[]{:S(2)}) collective-permute-start(bf16[128,2048]{1,0:T(8,128)(2,1)} %bitcast.117), channel_id=1, source_target_pairs={{0,1},{1,0},{2,3},{3,2},{4,5},{5,4},{6,7},{7,6},{8,9},{9,8},{10,11... | collective-permute-start | bytes 1572872 | tf_op jit(solution)/shard_map/ppermute | solution.py:347
  20.0 44.0 %all-to-all-start = ((bf16[8,64,512]{2,1,0:T(8,128)(2,1)}), bf16[8,64,512]{2,1,0:T(8,128)(2,1)S(1)}, u32[]{:S(2)}, u32[]{:S(2)}) async-start(bf16[8,64,512]{2,1,0:T(8,128)(2,1)} %squeeze.29), calls=%async_computation | async-start | bytes 1048576 | tf_op jit(solution)/shard_map/all_to_all | solution.py:495
  49.4 26.1 %collective-permute-start.11 = (bf16[128,2048]{1,0:T(8,128)(2,1)}, bf16[128,2048]{1,0:T(8,128)(2,1)}, u32[]{:S(2)}, u32[]{:S(2)}) collective-permute-start(bf16[128,2048]{1,0:T(8,128)(2,1)} %collective-permute-done), channel_id=1, source_target_pairs={{2,4},{3,5},{4,6},{5,7},{10,12},{11,13},{12,14},{13,15},{18,20},{1... | collective-permute-start | bytes 1572872 | tf_op jit(solution)/shard_map/ppermute | solution.py:342
  59.9 33.6 %collective-permute-start.12 = (bf16[128,2048]{1,0:T(8,128)(2,1)}, bf16[128,2048]{1,0:T(8,128)(2,1)}, u32[]{:S(2)}, u32[]{:S(2)}) collective-permute-start(bf16[128,2048]{1,0:T(8,128)(2,1)} %collective-permute-done.1), channel_id=1, source_target_pairs={{2,0},{3,1},{4,2},{5,3},{10,8},{11,9},{12,10},{13,11},{18,16},{19,... | collective-permute-start | bytes 1572872 | tf_op jit(solution)/shard_map/ppermute | solution.py:342
  62.6 35.0 %collective-permute-start.19 = (bf16[128,2048]{1,0:T(8,128)(2,1)}, bf16[128,2048]{1,0:T(8,128)(2,1)}, u32[]{:S(2)}, u32[]{:S(2)}) collective-permute-start(bf16[128,2048]{1,0:T(8,128)(2,1)} %param.24), channel_id=1, source_target_pairs={{0,8},{8,0},{16,24},{24,16},{1,9},{9,1},{17,25},{25,17},{2,10},{10... | collective-permute-start | bytes 1572872 | tf_op jit(solution)/shard_map/ppermute | solution.py:302
  64.0 71.1 %all-to-all-start.1 = ((bf16[8,64,512]{2,1,0:T(8,128)(2,1)}), bf16[8,64,512]{2,1,0:T(8,128)(2,1)}, u32[]{:S(2)}, u32[]{:S(2)}) async-start(bf16[8,64,512]{2,1,0:T(8,128)(2,1)} %squeeze.30), calls=%async_computation.1 | async-start | bytes 1048576 | tf_op jit(solution)/shard_map/all_to_all | solution.py:497
  71.5 27.4 %collective-permute-start.20 = (bf16[128,2048]{1,0:T(8,128)(2,1)}, bf16[128,2048]{1,0:T(8,128)(2,1)S(1)}, u32[]{:S(2)}, u32[]{:S(2)}) collective-permute-start(bf16[128,2048]{1,0:T(8,128)(2,1)} %param.24), channel_id=1, source_target_pairs={{0,16},{8,24},{16,0},{24,8},{1,17},{9,25},{17,1},{25,9},{2,18},{10... | collective-permute-start | bytes 1572872 | tf_op jit(solution)/shard_map/ppermute | solution.py:309
  73.6 27.0 %collective-permute-start.6 = (bf16[512,512]{1,0:T(8,128)(2,1)S(1)}, bf16[512,512]{1,0:T(8,128)(2,1)S(1)}, u32[]{:S(2)}, u32[]{:S(2)}) collective-permute-start(bf16[512,512]{1,0:T(8,128)(2,1)S(1)} %bitcast.119), channel_id=1, source_target_pairs={{0,8},{8,0},{16,24},{24,16},{1,9},{9,1},{17,25},{25,17},{2,10},{10... | collective-permute-start | bytes 1572872 | tf_op jit(solution)/shard_map/ppermute | solution.py:302
  95.5 36.6 %collective-permute-start.13 = (bf16[128,2048]{1,0:T(8,128)(2,1)S(1)}, bf16[128,2048]{1,0:T(8,128)(2,1)S(1)}, u32[]{:S(2)}, u32[]{:S(2)}) collective-permute-start(bf16[128,2048]{1,0:T(8,128)(2,1)S(1)} %get-tuple-element.126), channel_id=1, source_target_pairs={{0,1},{1,0},{2,3},{3,2},{4,5},{5,4},{6,7},{7,6},{8,9},{9,8},{10,11... | collective-permute-start | bytes 1572872 | tf_op jit(solution)/shard_map/ppermute | solution.py:347
  97.6 32.4 %collective-permute-start.14 = (bf16[128,2048]{1,0:T(8,128)(2,1)S(1)}, bf16[128,2048]{1,0:T(8,128)(2,1)}, u32[]{:S(2)}, u32[]{:S(2)}) collective-permute-start(bf16[128,2048]{1,0:T(8,128)(2,1)S(1)} %get-tuple-element.126), channel_id=1, source_target_pairs={{4,6},{5,7},{2,0},{3,1},{12,14},{13,15},{10,8},{11,9},{20,22},{21,... | collective-permute-start | bytes 1572872 | tf_op jit(solution)/shard_map/ppermute | solution.py:342
  98.9 41.5 %collective-permute-start.21 = (bf16[128,2048]{1,0:T(8,128)(2,1)S(1)}, bf16[128,2048]{1,0:T(8,128)(2,1)}, u32[]{:S(2)}, u32[]{:S(2)}) collective-permute-start(bf16[128,2048]{1,0:T(8,128)(2,1)S(1)} %collective-permute-done.20), channel_id=1, source_target_pairs={{0,8},{8,0},{16,24},{24,16},{1,9},{9,1},{17,25},{25,17},{2,10},{10... | collective-permute-start | bytes 1572872 | tf_op jit(solution)/shard_map/ppermute | solution.py:302
  100.1 47.4 %collective-permute-start.8 = (bf16[512,512]{1,0:T(8,128)(2,1)}, bf16[512,512]{1,0:T(8,128)(2,1)}, u32[]{:S(2)}, u32[]{:S(2)}) collective-permute-start(bf16[512,512]{1,0:T(8,128)(2,1)} %collective-permute-done.7), channel_id=1, source_target_pairs={{0,8},{8,0},{16,24},{24,16},{1,9},{9,1},{17,25},{25,17},{2,10},{10... | collective-permute-start | bytes 1572872 | tf_op jit(solution)/shard_map/ppermute | solution.py:302
  162.9 25.9 %all-to-all-start.3 = ((bf16[8,128,160]{1,2,0:T(8,128)(2,1)}), bf16[8,128,160]{1,2,0:T(8,128)(2,1)S(1)}, u32[]{:S(2)}, u32[]{:S(2)}) async-start(bf16[8,128,160]{1,2,0:T(8,128)(2,1)} %copy_bitcast_fusion.4), calls=%async_computation.3 | async-start | bytes 655360 | tf_op jit(solution)/shard_map/all_to_all | solution.py:446
  194.3 143.7 %reduce-scatter.4.cloned.1.call-start = ((), (), s32[]{:S(2)}) async-start(), calls=%async_computation.12 | async-start | bytes 4718592 | tf_op jit(solution)/shard_map/reduce_scatter | solution.py:573
  246.5 39.6 %collective-permute-start.22 = (bf16[512,512]{1,0:T(8,128)(2,1)}, bf16[512,512]{1,0:T(8,128)(2,1)}, u32[]{:S(2)}, u32[]{:S(2)}) collective-permute-start(bf16[512,512]{1,0:T(8,128)(2,1)} %get-tuple-element.138), channel_id=1, source_target_pairs={{0,8},{8,0},{16,24},{24,16},{1,9},{9,1},{17,25},{25,17},{2,10},{10... | collective-permute-start | bytes 1572872 | tf_op jit(solution)/shard_map/ppermute | solution.py:302
  315.8 31.0 %all-to-all-start.7 = ((bf16[8,64,512]{2,1,0:T(8,128)(2,1)}), bf16[8,64,512]{2,1,0:T(8,128)(2,1)S(1)}, u32[]{:S(2)}, u32[]{:S(2)}) async-start(bf16[8,64,512]{2,1,0:T(8,128)(2,1)} %bitcast.27), calls=%async_computation.8 | async-start | bytes 1048576 | tf_op jit(solution)/shard_map/all_to_all | solution.py:622
  319.8 83.9 %reduce-scatter.6.cloned.1.call-start = ((), (), s32[]{:S(2)}) async-start(), calls=%async_computation.13 | async-start | bytes 798720 | tf_op jit(solution)/shard_map/reduce_scatter | solution.py:643
  329.9 98.3 %reduce-scatter.8.cloned.1.call-start = ((), (), s32[]{:S(2)}) async-start(), calls=%async_computation.14 | async-start | bytes 2621440 | tf_op jit(solution)/shard_map/reduce_scatter | solution.py:624
  353.5 24.8 %collective-permute-start.27 = (bf16[128,2048]{1,0:T(8,128)(2,1)}, bf16[128,2048]{1,0:T(8,128)(2,1)}, u32[]{:S(2)}, u32[]{:S(2)}) collective-permute-start(bf16[128,2048]{1,0:T(8,128)(2,1)} %get-tuple-element.133), channel_id=1, source_target_pairs={{0,1},{1,0},{2,3},{3,2},{4,5},{5,4},{6,7},{7,6},{8,9},{9,8},{10,11... | collective-permute-start | bytes 1572872 | tf_op jit(solution)/shard_map/ppermute | solution.py:347
  354.0 34.6 %collective-permute-start.28 = (bf16[128,2048]{1,0:T(8,128)(2,1)}, bf16[128,2048]{1,0:T(8,128)(2,1)}, u32[]{:S(2)}, u32[]{:S(2)}) collective-permute-start(bf16[128,2048]{1,0:T(8,128)(2,1)} %get-tuple-element.132), channel_id=1, source_target_pairs={{0,1},{1,0},{2,3},{3,2},{4,5},{5,4},{8,9},{9,8},{10,11},{11,10},{1... | collective-permute-start | bytes 1572872 | tf_op jit(solution)/shard_map/ppermute | solution.py:347
  357.5 32.7 %collective-permute-start.29 = (bf16[128,2048]{1,0:T(8,128)(2,1)}, bf16[128,2048]{1,0:T(8,128)(2,1)}, u32[]{:S(2)}, u32[]{:S(2)}) collective-permute-start(bf16[128,2048]{1,0:T(8,128)(2,1)} %get-tuple-element.131), channel_id=1, source_target_pairs={{2,3},{3,2},{4,5},{5,4},{6,7},{7,6},{10,11},{11,10},{12,13},{13,12... | collective-permute-start | bytes 1572872 | tf_op jit(solution)/shard_map/ppermute | solution.py:347
  370.8 25.6 %collective-permute-start.35 = (bf16[512,512]{1,0:T(8,128)(2,1)S(1)}, bf16[512,512]{1,0:T(8,128)(2,1)S(1)}, u32[]{:S(2)}, u32[]{:S(2)}) collective-permute-start(bf16[512,512]{1,0:T(8,128)(2,1)S(1)} %get-tuple-element.137), channel_id=1, source_target_pairs={{0,8},{8,0},{16,24},{24,16},{1,9},{9,1},{17,25},{25,17},{2,10},{10... | collective-permute-start | bytes 1572872 | tf_op jit(solution)/shard_map/ppermute | solution.py:302
  (81 other events, 1286.6 us)
Sparse Core Ops, SparseCore 0:
  10.1 109.9 all-gather.2
  236.1 101.8 reduce-scatter.3
  340.7 20.5 reduce-scatter.5
  365.3 37.5 reduce-scatter.7
